TPU v7x, 32 devices: a whole 2x2x4 slice. The times are simulated.
32 devices in a mesh: dp: 2 (over x), expert: 16 (over z, y, core).
Axes of the slice: x: 2, y: 2, z: 4, core: 2. Of those that a mesh axis runs over, the one named last changes fastest.
Arguments:
- tokens: bfloat16 [4096, 2048], P(('dp', 'expert')), may hold values from -6 to 6
- cotangent: bfloat16 [4096, 2048], P(('dp', 'expert')), may hold values from -6 to 6
- expert_ids: int32 [4096, 8], P(('dp', 'expert')), may hold values from 0 to 127, as said below
- gate_probs: float32 [4096, 8], P(('dp', 'expert')), may hold values from 0.1 to 1
- gate_weight: bfloat16 [16, 2048, 128], P('expert'), may hold values from -0.125 to 0.125
- up_weight: bfloat16 [16, 2048, 128], P('expert'), may hold values from -0.125 to 0.125
- down_weight: bfloat16 [16, 128, 2048], P('expert'), may hold values from -0.1875 to 0.1875
Outputs:
- grad_input: bfloat16 [4096, 2048], P(('dp', 'expert'))
- grad_gate: bfloat16 [16, 2048, 128], P('expert')
- grad_up: bfloat16 [16, 2048, 128], P('expert')
- grad_down: bfloat16 [16, 128, 2048], P('expert')
Inputs may be any that keep to these rules, and one draw needn't show every extreme that they name: `expert_ids`: each row names 8 different experts. Among the 128 rows of one device, each window expert 0 to 1 is named by 1 to 8 rows, and in every draw one window expert of every device is named by exactly 8 rows.
All inputs are finite; a program needn't handle non-finite values.
Results may differ from a plain program's by a relative error of at most 0.0064.
Values may be sent and summed in bfloat16 or wider, within the bound.
No kernel may reach another device: no remote copies, remote signals or barrier semaphores. Data moves between devices by JAX's collectives and lax.ppermute only.
A program may use at most 64 MiB of HBM per device.

v0:
```python
import functools

import jax
import jax.numpy as jnp
from jax import lax
from jax.experimental import pallas as pl
from jax.experimental.pallas import tpu as pltpu
from jax.sharding import Mesh, PartitionSpec as P


SLICES = 8
CAP = 8
FAR = 4


NT = (((1,), (1,)), ((), ()))
TN = (((0,), (0,)), ((), ()))


def silu_parts(gate_pre):
    sigmoid_value = jax.nn.sigmoid(gate_pre)
    return (gate_pre * sigmoid_value, sigmoid_value * (1.0 + gate_pre * (1.0 - sigmoid_value)))


def hidden(rows, gate_rows, up_rows, down_rows):
    width = gate_rows.shape[0]
    rows_in, rows_cot = rows[:, :width], rows[:, width:]
    gate_pre = jnp.dot(rows_in, gate_rows, preferred_element_type=jnp.float32)
    upward = jnp.dot(rows_in, up_rows, preferred_element_type=jnp.float32)
    dhidden = lax.dot_general(rows_cot, down_rows, NT, preferred_element_type=jnp.float32)
    swish, slope = silu_parts(gate_pre)
    active = (swish * upward).astype(jnp.bfloat16)
    dgate = (dhidden * upward * slope).astype(jnp.bfloat16)
    dupward = (dhidden * swish).astype(jnp.bfloat16)
    return active, dgate, dupward


def part_of(hid, gate_rows, up_rows):
    value = lax.dot_general(hid[1], gate_rows, NT, preferred_element_type=jnp.float32)
    return value + lax.dot_general(hid[2], up_rows, NT, preferred_element_type=jnp.float32)


def weight_grads(rows, hid):
    active, dgate, dupward = hid
    width = rows.shape[1] // 2
    rows_in, rows_cot = rows[:, :width], rows[:, width:]
    return (
        lax.dot_general(rows_in, dgate, TN, preferred_element_type=jnp.float32),
        lax.dot_general(rows_in, dupward, TN, preferred_element_type=jnp.float32),
        lax.dot_general(active, rows_cot, TN, preferred_element_type=jnp.float32),
    )


def front_kernel(window, mine_ref, ids_hbm, probs_hbm, tokens_hbm, cot_hbm, rows_ref, picker_ref,
                 ids_ref, probs_ref, tokens_ref, cot_ref, sems):
    copies = [
        pltpu.make_async_copy(source, target, sems.at[index])
        for index, (source, target) in enumerate(
            (
                (ids_hbm, ids_ref),
                (probs_hbm, probs_ref),
                (tokens_hbm, tokens_ref),
                (cot_hbm, cot_ref),
            )
        )
    ]
    for copy in copies:
        copy.start()
    mine = mine_ref[0]
    count, width = tokens_ref.shape
    slots = window * CAP
    slot = lax.broadcasted_iota(jnp.int32, (slots, count), 0)
    earlier = lax.broadcasted_iota(jnp.int32, (count, count), 0) < lax.broadcasted_iota(
        jnp.int32, (count, count), 1
    )
    copies[0].wait()
    copies[1].wait()
    ids = ids_ref[...]
    probs = probs_ref[...]
    hit = jnp.zeros((slots, count), jnp.float32)
    chosen = jnp.zeros((slots, count), jnp.float32)
    for index in range(window):
        match = ids == (mine ^ index)
        hits = jnp.sum(match.astype(jnp.float32), axis=0, keepdims=True)
        prob = jnp.sum(jnp.where(match, probs, 0.0), axis=0, keepdims=True)
        here = slot // CAP == index
        hit = jnp.where(here, hits, hit)
        chosen = jnp.where(here, prob, chosen)
    rank = jnp.dot(
        hit.astype(jnp.bfloat16), earlier.astype(jnp.bfloat16), preferred_element_type=jnp.float32
    )
    placed = (hit == 1.0) & (rank.astype(jnp.int32) == slot % CAP)
    picker = placed.astype(jnp.bfloat16)
    picker_ref[...] = picker
    prob = jnp.sum(jnp.where(placed, chosen, 0.0), axis=1, keepdims=True)
    copies[2].wait()
    rows_in = jnp.dot(picker, tokens_ref[...], preferred_element_type=jnp.float32)
    rows_ref[:, :width] = rows_in.astype(jnp.bfloat16)
    copies[3].wait()
    rows_cot = jnp.dot(picker, cot_ref[...], preferred_element_type=jnp.float32)
    rows_ref[:, width:] = (prob * rows_cot).astype(jnp.bfloat16)


def front(mine, ids, probs, tokens, cotangent, window):
    count, width = tokens.shape
    slots = window * CAP
    vmem = pl.BlockSpec(memory_space=pltpu.VMEM)
    away = pl.BlockSpec(memory_space=pltpu.HBM)
    return pl.pallas_call(
        functools.partial(front_kernel, window),
        out_shape=(
            jax.ShapeDtypeStruct((slots, 2 * width), jnp.bfloat16),
            jax.ShapeDtypeStruct((slots, count), jnp.bfloat16),
        ),
        in_specs=[pl.BlockSpec(memory_space=pltpu.SMEM), away, away, away, away],
        out_specs=(vmem, vmem),
        scratch_shapes=[
            pltpu.VMEM(ids.shape, ids.dtype),
            pltpu.VMEM(probs.shape, probs.dtype),
            pltpu.VMEM(tokens.shape, tokens.dtype),
            pltpu.VMEM(cotangent.shape, cotangent.dtype),
            pltpu.SemaphoreType.DMA((4,)),
        ],
        compiler_params=pltpu.CompilerParams(vmem_limit_bytes=8 << 20),
        name="front",
    )(mine, ids, probs, tokens, cotangent)


TILES = 8


def finish_kernel(gate_ref, up_ref, down_ref, rows_ref, active_ref, dgate_ref, dupward_ref,
                  gate_hbm, up_hbm, down_hbm, gate_out, up_out, down_out, sems):
    width = gate_ref.shape[0]
    tile = width // TILES
    copies = []

    def send(source, target, index):
        copy = pltpu.make_async_copy(source, target, sems.at[index])
        copy.start()
        copies.append(copy)

    for index in range(TILES):
        part = pl.ds(index * tile, tile)
        rows_in = rows_ref[:, index * tile : (index + 1) * tile]
        rows_cot = rows_ref[:, width + index * tile : width + (index + 1) * tile]
        for source, slope, out, hbm, sem in (
            (gate_ref, dgate_ref, gate_out, gate_hbm, 0),
            (up_ref, dupward_ref, up_out, up_hbm, 1),
        ):
            more = lax.dot_general(rows_in, slope[...], TN, preferred_element_type=jnp.float32)
            out[part, :] = (source[part, :] + more).astype(jnp.bfloat16)
            send(out.at[part, :], hbm.at[part, :], 3 * index + sem)
        more = lax.dot_general(active_ref[...], rows_cot, TN, preferred_element_type=jnp.float32)
        down_out[:, part] = (down_ref[:, part] + more).astype(jnp.bfloat16)
        send(down_out.at[:, part], down_hbm.at[:, part], 3 * index + 2)
    for copy in copies:
        copy.wait()


def finish(grads, rows, hid):
    vmem = pl.BlockSpec(memory_space=pltpu.VMEM)
    away = pl.BlockSpec(memory_space=pltpu.HBM)
    return pl.pallas_call(
        finish_kernel,
        out_shape=tuple(jax.ShapeDtypeStruct(g.shape, jnp.bfloat16) for g in grads),
        in_specs=[vmem] * 7,
        out_specs=(away,) * 3,
        scratch_shapes=[pltpu.VMEM(g.shape, jnp.bfloat16) for g in grads]
        + [pltpu.SemaphoreType.DMA((3 * TILES,))],
        compiler_params=pltpu.CompilerParams(vmem_limit_bytes=12 << 20),
        name="finish",
    )(*grads, rows, *hid)


def local(tokens, cotangent, expert_ids, gate_probs, gate_weight, up_weight, down_weight):
    groups = lax.axis_size("dp")
    window = lax.axis_size("win")
    mine = lax.axis_index("win")
    weights = (gate_weight[0], up_weight[0], down_weight[0])
    block = window * CAP

    def swap(value, axis, mask):
        pairs = [(i, i ^ mask) for i in range(lax.axis_size(axis))]
        return lax.ppermute(value, axis, pairs)

    def join(items):
        return jnp.concatenate(items, axis=0)

    rows, picker = front(
        mine.astype(jnp.int32)[None], expert_ids.T, gate_probs.T, tokens, cotangent, window
    )
    held = [rows[:CAP]]
    for index in range(1, window):
        held.append(swap(rows[index * CAP : (index + 1) * CAP], "win", index))

    rows = {0: join(held)}
    for mask in (6, 4, 2):
        rows[mask] = swap(rows[0], "slice", mask)
    for mask in (0, 2, 6, 4):
        rows[mask + 1] = swap(rows[mask], "slice", 1)

    def pair(mask):
        return join([rows[mask], rows[mask ^ FAR]])

    even = join([pair(0), pair(2)])
    hid_even = hidden(even, *weights)
    part = part_of(hid_even, *weights[:2])
    back = part[: 2 * block]
    part = part[2 * block :].astype(jnp.bfloat16)
    incoming = [swap(part, "slice", 2)]
    piece, _ = lax.optimization_barrier((pair(3), part))
    hid_three = hidden(piece, *weights)
    part = part_of(hid_three, *weights[:2]).astype(jnp.bfloat16)
    incoming.append(swap(part, "slice", 3))
    piece, _ = lax.optimization_barrier((pair(1), part))
    hid_one = hidden(piece, *weights)
    part = part_of(hid_one, *weights[:2]).astype(jnp.bfloat16)
    incoming.append(swap(part, "slice", 1))
    last = part
    for part in incoming:
        back = back + part.astype(jnp.float32)

    far = swap(back[block:].astype(jnp.bfloat16), "slice", FAR)
    back = (back[:block] + far.astype(jnp.float32)).astype(jnp.bfloat16)
    kept = [back[:CAP]]
    for index in range(1, window):
        kept.append(swap(back[index * CAP : (index + 1) * CAP], "win", index))
    grad_input = lax.dot_general(
        picker, join(kept), TN, preferred_element_type=jnp.float32
    ).astype(jnp.bfloat16)

    hid = [join(items) for items in zip(hid_even, hid_three, hid_one)]
    grads = weight_grads(join([even, pair(3), pair(1)]), hid)
    grads = lax.optimization_barrier(grads)
    for mask in range(1, groups):
        pieces = [rows[0], join([rows[2], rows[4], rows[6]]), pair(3), pair(1)]
        if mask > 1:
            pieces, grads = lax.optimization_barrier((pieces, grads))
        theirs = [swap(piece, "dp", mask) for piece in pieces]
        early, _ = lax.optimization_barrier((theirs[:-1], last))
        early = join(early)
        more = weight_grads(early, hidden(early, *weights))
        grads = tuple(a + b for a, b in zip(grads, more))
        late, _ = lax.optimization_barrier((theirs[-1], grad_input))
        hid = hidden(late, *weights)
        if mask < groups - 1:
            more = weight_grads(late, hid)
            grads = tuple(a + b for a, b in zip(grads, more))
    grads = finish(grads, late, hid)
    return (grad_input,) + tuple(g[None] for g in grads)


def solution(mesh):
    groups, devices = mesh.shape["dp"], mesh.shape["expert"]
    shape = (groups, SLICES, devices // SLICES)
    fine = Mesh(mesh.devices.reshape(shape), ("dp", "slice", "win"))
    rows = P(("dp", "slice", "win"), None)
    weight = P(("slice", "win"), None, None)
    return jax.shard_map(
        local,
        mesh=fine,
        in_specs=(rows, rows, rows, rows, weight, weight, weight),
        out_specs=(rows, weight, weight, weight),
        check_vma=False,
    )
```

profile of v0, /device:TPU:0, one launch (start us, length us, event | category | flops | bytes accessed | tf_op | source)
XLA Modules:
  0.0 62.6 jit_solution(9144408969030198755)
XLA Ops:
  1.4 1.0 %copy-done.1 = bf16[128,2048]{1,0:T(8,128)(2,1)S(1)} copy-done((bf16[128,2048]{1,0:T(8,128)(2,1)S(1)}, bf16[128,2048]{1,0:T(8,128)(2,1)}, u32[]{:S(2)}) %copy-start.1) | copy-done | bytes 524312
  2.5 1.0 %copy-done.2 = bf16[128,2048]{1,0:T(8,128)(2,1)S(1)} copy-done((bf16[128,2048]{1,0:T(8,128)(2,1)S(1)}, bf16[128,2048]{1,0:T(8,128)(2,1)}, u32[]{:S(2)}) %copy-start.2) | copy-done | bytes 524312
  5.7 4.0 %collective-permute-start.1 = (bf16[16,4096]{1,0:T(8,128)(2,1)S(1)}, bf16[16,4096]{1,0:T(8,128)(2,1)S(1)}, u32[]{:S(2)}, u32[]{:S(2)}) collective-permute-start(bf16[16,4096]{1,0:T(8,128)(2,1)S(1)} %pad_maximum_fusion.1), channel_id=1, source_target_pairs={{0,8},{2,10},{4,12},{6,14},{8,0},{10,2},{12,4},{14,6},{1,9},{3,11}... | collective-permute-start | bytes 393224 | tf_op jit(solution)/shard_map/ppermute | solution.py:185
  9.7 1.6 %collective-permute-start.2 = (bf16[16,4096]{1,0:T(8,128)(2,1)S(1)}, bf16[16,4096]{1,0:T(8,128)(2,1)S(1)}, u32[]{:S(2)}, u32[]{:S(2)}) collective-permute-start(bf16[16,4096]{1,0:T(8,128)(2,1)S(1)} %pad_maximum_fusion.1), channel_id=1, source_target_pairs={{0,4},{2,6},{4,0},{6,2},{8,12},{10,14},{12,8},{14,10},{1,5},{3,7},... | collective-permute-start | bytes 393224 | tf_op jit(solution)/shard_map/ppermute | solution.py:185
  11.3 1.7 %collective-permute-start.8 = (bf16[16,4096]{1,0:T(8,128)(2,1)S(1)}, bf16[16,4096]{1,0:T(8,128)(2,1)S(1)}, u32[]{:S(2)}, u32[]{:S(2)}) collective-permute-start(bf16[16,4096]{1,0:T(8,128)(2,1)S(1)} %pad_maximum_fusion.1), channel_id=1, source_target_pairs={{0,2},{2,0},{4,6},{6,4},{8,10},{10,8},{12,14},{14,12},{1,3},{3,1},... | collective-permute-start | bytes 393224 | tf_op jit(solution)/shard_map/ppermute | solution.py:185
  13.0 1.5 %collective-permute-start.13 = (bf16[16,4096]{1,0:T(8,128)(2,1)S(1)}, bf16[16,4096]{1,0:T(8,128)(2,1)S(1)}, u32[]{:S(2)}, u32[]{:S(2)}) collective-permute-start(bf16[16,4096]{1,0:T(8,128)(2,1)S(1)} %pad_maximum_fusion.1), channel_id=1, source_target_pairs={{0,16},{16,0},{1,17},{17,1},{2,18},{18,2},{3,19},{19,3},{4,20},{20... | collective-permute-start | bytes 393224 | tf_op jit(solution)/shard_map/ppermute | solution.py:185
  14.5 2.6 %collective-permute-done.1 = bf16[16,4096]{1,0:T(8,128)(2,1)S(1)} collective-permute-done((bf16[16,4096]{1,0:T(8,128)(2,1)S(1)}, bf16[16,4096]{1,0:T(8,128)(2,1)S(1)}, u32[]{:S(2)}, u32[]{:S(2)}) %collective-permute-start.1) | collective-permute-done | bytes 131104 | tf_op jit(solution)/shard_map/ppermute | solution.py:185
  17.2 3.2 %collective-permute-done.3 = bf16[16,4096]{1,0:T(8,128)(2,1)S(1)} collective-permute-done((bf16[16,4096]{1,0:T(8,128)(2,1)S(1)}, bf16[16,4096]{1,0:T(8,128)(2,1)S(1)}, u32[]{:S(2)}, u32[]{:S(2)}) %collective-permute-start.3) | collective-permute-done | bytes 131104 | tf_op jit(solution)/shard_map/ppermute | solution.py:185
  22.6 2.4 %collective-permute-start.4 = (bf16[32,2048]{1,0:T(8,128)(2,1)S(1)}, bf16[32,2048]{1,0:T(8,128)(2,1)S(1)}, u32[]{:S(2)}, u32[]{:S(2)}) collective-permute-start(bf16[32,2048]{1,0:T(8,128)(2,1)S(1)} %slice.150), channel_id=1, source_target_pairs={{0,4},{2,6},{4,0},{6,2},{8,12},{10,14},{12,8},{14,10},{1,5},{3,7},... | collective-permute-start | bytes 393224 | tf_op jit(solution)/shard_map/ppermute | solution.py:185
  25.0 1.5 %collective-permute-start.5 = (bf16[16,4096]{1,0:T(8,128)(2,1)S(1)}, bf16[16,4096]{1,0:T(8,128)(2,1)S(1)}, u32[]{:S(2)}, u32[]{:S(2)}) collective-permute-start(bf16[16,4096]{1,0:T(8,128)(2,1)S(1)} %collective-permute-done.2), channel_id=1, source_target_pairs={{0,2},{2,0},{4,6},{6,4},{8,10},{10,8},{12,14},{14,12},{1,3},{3,1},... | collective-permute-start | bytes 393224 | tf_op jit(solution)/shard_map/ppermute | solution.py:185
  26.5 1.6 %collective-permute-start.14 = (bf16[48,4096]{1,0:T(8,128)(2,1)S(1)}, bf16[48,4096]{1,0:T(8,128)(2,1)S(1)}, u32[]{:S(2)}, u32[]{:S(2)}) collective-permute-start(bf16[48,4096]{1,0:T(8,128)(2,1)S(1)} %pad_maximum_fusion), channel_id=1, source_target_pairs={{0,16},{16,0},{1,17},{17,1},{2,18},{18,2},{3,19},{19,3},{4,20},{20... | collective-permute-start | bytes 1179656 | tf_op jit(solution)/shard_map/ppermute | solution.py:185
  28.1 2.0 %collective-permute-done.5 = bf16[16,4096]{1,0:T(8,128)(2,1)S(1)} collective-permute-done((bf16[16,4096]{1,0:T(8,128)(2,1)S(1)}, bf16[16,4096]{1,0:T(8,128)(2,1)S(1)}, u32[]{:S(2)}, u32[]{:S(2)}) %collective-permute-start.5) | collective-permute-done | bytes 131104 | tf_op jit(solution)/shard_map/ppermute | solution.py:185
  30.1 1.5 %collective-permute-start.6 = (bf16[16,4096]{1,0:T(8,128)(2,1)S(1)}, bf16[16,4096]{1,0:T(8,128)(2,1)S(1)}, u32[]{:S(2)}, u32[]{:S(2)}) collective-permute-start(bf16[16,4096]{1,0:T(8,128)(2,1)S(1)} %collective-permute-done.3), channel_id=1, source_target_pairs={{0,2},{2,0},{4,6},{6,4},{8,10},{10,8},{12,14},{14,12},{1,3},{3,1},... | collective-permute-start | bytes 393224 | tf_op jit(solution)/shard_map/ppermute | solution.py:185
  31.7 3.4 %collective-permute-done.6 = bf16[16,4096]{1,0:T(8,128)(2,1)S(1)} collective-permute-done((bf16[16,4096]{1,0:T(8,128)(2,1)S(1)}, bf16[16,4096]{1,0:T(8,128)(2,1)S(1)}, u32[]{:S(2)}, u32[]{:S(2)}) %collective-permute-start.6) | collective-permute-done | bytes 131104 | tf_op jit(solution)/shard_map/ppermute | solution.py:185
  35.1 1.5 %collective-permute-start.9 = (bf16[16,4096]{1,0:T(8,128)(2,1)S(1)}, bf16[16,4096]{1,0:T(8,128)(2,1)S(1)}, u32[]{:S(2)}, u32[]{:S(2)}) collective-permute-start(bf16[16,4096]{1,0:T(8,128)(2,1)S(1)} %collective-permute-done.1), channel_id=1, source_target_pairs={{0,2},{2,0},{4,6},{6,4},{8,10},{10,8},{12,14},{14,12},{1,3},{3,1},... | collective-permute-start | bytes 393224 | tf_op jit(solution)/shard_map/ppermute | solution.py:185
  37.9 2.1 %collective-permute-done.9 = bf16[16,4096]{1,0:T(8,128)(2,1)S(1)} collective-permute-done((bf16[16,4096]{1,0:T(8,128)(2,1)S(1)}, bf16[16,4096]{1,0:T(8,128)(2,1)S(1)}, u32[]{:S(2)}, u32[]{:S(2)}) %collective-permute-start.9) | collective-permute-done | bytes 131104 | tf_op jit(solution)/shard_map/ppermute | solution.py:185
  40.6 1.3 %collective-permute-start.7 = (bf16[32,2048]{1,0:T(8,128)(2,1)S(1)}, bf16[32,2048]{1,0:T(8,128)(2,1)S(1)}, u32[]{:S(2)}, u32[]{:S(2)}) collective-permute-start(bf16[32,2048]{1,0:T(8,128)(2,1)S(1)} %fusion), channel_id=1, source_target_pairs={{0,6},{2,4},{4,2},{6,0},{8,14},{10,12},{12,10},{14,8},{1,7},{3,5},... | collective-permute-start | bytes 393224 | tf_op jit(solution)/shard_map/ppermute | solution.py:185
  43.6 1.6 %collective-permute-start.16 = (bf16[32,4096]{1,0:T(8,128)(2,1)S(1)}, bf16[32,4096]{1,0:T(8,128)(2,1)S(1)}, u32[]{:S(2)}, u32[]{:S(2)}) collective-permute-start(bf16[32,4096]{1,0:T(8,128)(2,1)S(1)} %get-tuple-element.21), channel_id=1, source_target_pairs={{0,16},{16,0},{1,17},{17,1},{2,18},{18,2},{3,19},{19,3},{4,20},{20... | collective-permute-start | bytes 786440 | tf_op jit(solution)/shard_map/ppermute | solution.py:185
  45.2 2.7 %collective-permute-done.10 = bf16[32,2048]{1,0:T(8,128)(2,1)S(1)} collective-permute-done((bf16[32,2048]{1,0:T(8,128)(2,1)S(1)}, bf16[32,2048]{1,0:T(8,128)(2,1)S(1)}, u32[]{:S(2)}, u32[]{:S(2)}) %collective-permute-start.10) | collective-permute-done | bytes 131104 | tf_op jit(solution)/shard_map/ppermute | solution.py:185
  47.9 1.5 %collective-permute-start.15 = (bf16[32,4096]{1,0:T(8,128)(2,1)S(1)}, bf16[32,4096]{1,0:T(8,128)(2,1)S(1)}, u32[]{:S(2)}, u32[]{:S(2)}) collective-permute-start(bf16[32,4096]{1,0:T(8,128)(2,1)S(1)} %get-tuple-element.20), channel_id=1, source_target_pairs={{0,16},{16,0},{1,17},{17,1},{2,18},{18,2},{3,19},{19,3},{4,20},{20... | collective-permute-start | bytes 786440 | tf_op jit(solution)/shard_map/ppermute | solution.py:185
  49.4 3.5 %collective-permute-start.11 = (bf16[16,2048]{1,0:T(8,128)(2,1)S(1)}, bf16[16,2048]{1,0:T(8,128)(2,1)S(1)}, u32[]{:S(2)}, u32[]{:S(2)}) collective-permute-start(bf16[16,2048]{1,0:T(8,128)(2,1)S(1)} %slice.151), channel_id=1, source_target_pairs={{0,8},{2,10},{4,12},{6,14},{8,0},{10,2},{12,4},{14,6},{1,9},{3,11}... | collective-permute-start | bytes 196616 | tf_op jit(solution)/shard_map/ppermute | solution.py:185
  53.3 2.6 %collective-permute-done.11 = bf16[16,2048]{1,0:T(8,128)(2,1)S(1)} collective-permute-done((bf16[16,2048]{1,0:T(8,128)(2,1)S(1)}, bf16[16,2048]{1,0:T(8,128)(2,1)S(1)}, u32[]{:S(2)}, u32[]{:S(2)}) %collective-permute-start.11) | collective-permute-done | bytes 65568 | tf_op jit(solution)/shard_map/ppermute | solution.py:185
  57.2 1.1 %convolution_convert_fusion = bf16[128,2048]{1,0:T(8,128)(2,1)} fusion(bf16[16,128]{1,0:T(8,128)(2,1)S(1)} %get-tuple-element.18, bf16[8,2048]{1,0:T(8,128)(2,1)S(1)} %collective-permute-done.12, bf16[8,2048]{1,0:T(8,128)(2,1)S(1)} %get-tuple-element.55), kind=kOutput, calls=%fused_computation.3 | convolution fusion | flops 8781824 | bytes 593920 | tf_op jit(solution)/shard_map/dot_general | solution.py:229
  61.0 1.6 %finish.1 = (bf16[2048,128]{1,0:T(8,128)(2,1)}, bf16[2048,128]{1,0:T(8,128)(2,1)}, bf16[128,2048]{1,0:T(8,128)(2,1)}) custom-call(f32[2048,128]{1,0:T(8,128)S(1)} %convolution_add_fusion.2.gate_ref, f32[2048,128]{1,0:T(8,128)S(1)} %convolution_add_fusion.1.up_ref, f32[128,2048]{1,0:T(8,128)S(1)} %convolution_add_fusion.down_ref, ...), custom_call_target="tpu_custom_call" | custom-call | tf_op jit(solution)/shard_map/finish/pallas_call | solution.py:164
  (73 shorter events, 13.0 us)
Async XLA Ops:
  0.6 21.1 %copy-start = (bf16[1,2048,128]{2,1,0:T(8,128)(2,1)S(1)}, bf16[1,2048,128]{2,1,0:T(8,128)(2,1)}, u32[]{:S(2)}) copy-start(bf16[1,2048,128]{2,1,0:T(8,128)(2,1)} %param.12) | copy-start | bytes 1572868
  0.6 0.7 %copy-start.4 = (f32[128,8]{0,1:T(8,128)S(1)}, f32[128,8]{0,1:T(8,128)}, u32[]{:S(2)}) copy-start(f32[128,8]{0,1:T(8,128)} %param.10) | copy-start | bytes 12292
  0.7 0.8 %copy-start.3 = (s32[128,8]{0,1:T(8,128)S(1)}, s32[128,8]{0,1:T(8,128)}, u32[]{:S(2)}) copy-start(s32[128,8]{0,1:T(8,128)} %param.9) | copy-start | bytes 12292
  1.4 1.0 %copy-start.1 = (bf16[128,2048]{1,0:T(8,128)(2,1)S(1)}, bf16[128,2048]{1,0:T(8,128)(2,1)}, u32[]{:S(2)}) copy-start(bf16[128,2048]{1,0:T(8,128)(2,1)} %tokens_hbm.1) | copy-start | bytes 1572868
  2.5 1.0 %copy-start.2 = (bf16[128,2048]{1,0:T(8,128)(2,1)S(1)}, bf16[128,2048]{1,0:T(8,128)(2,1)}, u32[]{:S(2)}) copy-start(bf16[128,2048]{1,0:T(8,128)(2,1)} %cot_hbm.1) | copy-start | bytes 1572868
  4.2 1.5 %collective-permute-start = (bf16[8,4096]{1,0:T(8,128)(2,1)S(1)}, bf16[8,4096]{1,0:T(8,128)(2,1)S(1)}, u32[]{:S(2)}, u32[]{:S(2)}) collective-permute-start(bf16[8,4096]{1,0:T(8,128)(2,1)S(1)} %get-tuple-element.48), channel_id=1, source_target_pairs={{0,1},{1,0},{2,3},{3,2},{4,5},{5,4},{6,7},{7,6},{8,9},{9,8},{10,11... | collective-permute-start | bytes 196616 | tf_op jit(solution)/shard_map/ppermute | solution.py:185
  5.7 11.4 %collective-permute-start.1 = (bf16[16,4096]{1,0:T(8,128)(2,1)S(1)}, bf16[16,4096]{1,0:T(8,128)(2,1)S(1)}, u32[]{:S(2)}, u32[]{:S(2)}) collective-permute-start(bf16[16,4096]{1,0:T(8,128)(2,1)S(1)} %pad_maximum_fusion.1), channel_id=1, source_target_pairs={{0,8},{2,10},{4,12},{6,14},{8,0},{10,2},{12,4},{14,6},{1,9},{3,11}... | collective-permute-start | bytes 393224 | tf_op jit(solution)/shard_map/ppermute | solution.py:185
  9.7 7.4 %collective-permute-start.2 = (bf16[16,4096]{1,0:T(8,128)(2,1)S(1)}, bf16[16,4096]{1,0:T(8,128)(2,1)S(1)}, u32[]{:S(2)}, u32[]{:S(2)}) collective-permute-start(bf16[16,4096]{1,0:T(8,128)(2,1)S(1)} %pad_maximum_fusion.1), channel_id=1, source_target_pairs={{0,4},{2,6},{4,0},{6,2},{8,12},{10,14},{12,8},{14,10},{1,5},{3,7},... | collective-permute-start | bytes 393224 | tf_op jit(solution)/shard_map/ppermute | solution.py:185
  11.3 9.1 %collective-permute-start.3 = (bf16[16,4096]{1,0:T(8,128)(2,1)S(1)}, bf16[16,4096]{1,0:T(8,128)(2,1)S(1)}, u32[]{:S(2)}, u32[]{:S(2)}) collective-permute-start(bf16[16,4096]{1,0:T(8,128)(2,1)S(1)} %pad_maximum_fusion.1), channel_id=1, source_target_pairs={{0,12},{2,14},{4,8},{6,10},{8,4},{10,6},{12,0},{14,2},{1,13},{3,15... | collective-permute-start | bytes 393224 | tf_op jit(solution)/shard_map/ppermute | solution.py:185
  11.3 26.3 %collective-permute-start.8 = (bf16[16,4096]{1,0:T(8,128)(2,1)S(1)}, bf16[16,4096]{1,0:T(8,128)(2,1)S(1)}, u32[]{:S(2)}, u32[]{:S(2)}) collective-permute-start(bf16[16,4096]{1,0:T(8,128)(2,1)S(1)} %pad_maximum_fusion.1), channel_id=1, source_target_pairs={{0,2},{2,0},{4,6},{6,4},{8,10},{10,8},{12,14},{14,12},{1,3},{3,1},... | collective-permute-start | bytes 393224 | tf_op jit(solution)/shard_map/ppermute | solution.py:185
  13.0 45.7 %collective-permute-start.13 = (bf16[16,4096]{1,0:T(8,128)(2,1)S(1)}, bf16[16,4096]{1,0:T(8,128)(2,1)S(1)}, u32[]{:S(2)}, u32[]{:S(2)}) collective-permute-start(bf16[16,4096]{1,0:T(8,128)(2,1)S(1)} %pad_maximum_fusion.1), channel_id=1, source_target_pairs={{0,16},{16,0},{1,17},{17,1},{2,18},{18,2},{3,19},{19,3},{4,20},{20... | collective-permute-start | bytes 393224 | tf_op jit(solution)/shard_map/ppermute | solution.py:185
  17.1 3.3 %copy-start.5 = (bf16[1,2048,128]{2,1,0:T(8,128)(2,1)S(1)}, bf16[1,2048,128]{2,1,0:T(8,128)(2,1)}, u32[]{:S(2)}) copy-start(bf16[1,2048,128]{2,1,0:T(8,128)(2,1)} %param.11) | copy-start | bytes 1572868
  20.3 1.0 %copy-start.6 = (bf16[1,128,2048]{2,1,0:T(8,128)(2,1)S(1)}, bf16[1,128,2048]{2,1,0:T(8,128)(2,1)}, u32[]{:S(2)}) copy-start(bf16[1,128,2048]{2,1,0:T(8,128)(2,1)} %param.13) | copy-start | bytes 1572868
  22.6 21.0 %collective-permute-start.4 = (bf16[32,2048]{1,0:T(8,128)(2,1)S(1)}, bf16[32,2048]{1,0:T(8,128)(2,1)S(1)}, u32[]{:S(2)}, u32[]{:S(2)}) collective-permute-start(bf16[32,2048]{1,0:T(8,128)(2,1)S(1)} %slice.150), channel_id=1, source_target_pairs={{0,4},{2,6},{4,0},{6,2},{8,12},{10,14},{12,8},{14,10},{1,5},{3,7},... | collective-permute-start | bytes 393224 | tf_op jit(solution)/shard_map/ppermute | solution.py:185
  25.0 5.1 %collective-permute-start.5 = (bf16[16,4096]{1,0:T(8,128)(2,1)S(1)}, bf16[16,4096]{1,0:T(8,128)(2,1)S(1)}, u32[]{:S(2)}, u32[]{:S(2)}) collective-permute-start(bf16[16,4096]{1,0:T(8,128)(2,1)S(1)} %collective-permute-done.2), channel_id=1, source_target_pairs={{0,2},{2,0},{4,6},{6,4},{8,10},{10,8},{12,14},{14,12},{1,3},{3,1},... | collective-permute-start | bytes 393224 | tf_op jit(solution)/shard_map/ppermute | solution.py:185
  26.5 32.2 %collective-permute-start.14 = (bf16[48,4096]{1,0:T(8,128)(2,1)S(1)}, bf16[48,4096]{1,0:T(8,128)(2,1)S(1)}, u32[]{:S(2)}, u32[]{:S(2)}) collective-permute-start(bf16[48,4096]{1,0:T(8,128)(2,1)S(1)} %pad_maximum_fusion), channel_id=1, source_target_pairs={{0,16},{16,0},{1,17},{17,1},{2,18},{18,2},{3,19},{19,3},{4,20},{20... | collective-permute-start | bytes 1179656 | tf_op jit(solution)/shard_map/ppermute | solution.py:185
  30.1 5.0 %collective-permute-start.6 = (bf16[16,4096]{1,0:T(8,128)(2,1)S(1)}, bf16[16,4096]{1,0:T(8,128)(2,1)S(1)}, u32[]{:S(2)}, u32[]{:S(2)}) collective-permute-start(bf16[16,4096]{1,0:T(8,128)(2,1)S(1)} %collective-permute-done.3), channel_id=1, source_target_pairs={{0,2},{2,0},{4,6},{6,4},{8,10},{10,8},{12,14},{14,12},{1,3},{3,1},... | collective-permute-start | bytes 393224 | tf_op jit(solution)/shard_map/ppermute | solution.py:185
  35.1 5.0 %collective-permute-start.9 = (bf16[16,4096]{1,0:T(8,128)(2,1)S(1)}, bf16[16,4096]{1,0:T(8,128)(2,1)S(1)}, u32[]{:S(2)}, u32[]{:S(2)}) collective-permute-start(bf16[16,4096]{1,0:T(8,128)(2,1)S(1)} %collective-permute-done.1), channel_id=1, source_target_pairs={{0,2},{2,0},{4,6},{6,4},{8,10},{10,8},{12,14},{14,12},{1,3},{3,1},... | collective-permute-start | bytes 393224 | tf_op jit(solution)/shard_map/ppermute | solution.py:185
  40.6 8.8 %collective-permute-start.7 = (bf16[32,2048]{1,0:T(8,128)(2,1)S(1)}, bf16[32,2048]{1,0:T(8,128)(2,1)S(1)}, u32[]{:S(2)}, u32[]{:S(2)}) collective-permute-start(bf16[32,2048]{1,0:T(8,128)(2,1)S(1)} %fusion), channel_id=1, source_target_pairs={{0,6},{2,4},{4,2},{6,0},{8,14},{10,12},{12,10},{14,8},{1,7},{3,5},... | collective-permute-start | bytes 393224 | tf_op jit(solution)/shard_map/ppermute | solution.py:185
  42.7 5.2 %collective-permute-start.10 = (bf16[32,2048]{1,0:T(8,128)(2,1)S(1)}, bf16[32,2048]{1,0:T(8,128)(2,1)S(1)}, u32[]{:S(2)}, u32[]{:S(2)}) collective-permute-start(bf16[32,2048]{1,0:T(8,128)(2,1)S(1)} %fusion.1), channel_id=1, source_target_pairs={{0,2},{2,0},{4,6},{6,4},{8,10},{10,8},{12,14},{14,12},{1,3},{3,1},... | collective-permute-start | bytes 393224 | tf_op jit(solution)/shard_map/ppermute | solution.py:185
  43.6 14.7 %collective-permute-start.16 = (bf16[32,4096]{1,0:T(8,128)(2,1)S(1)}, bf16[32,4096]{1,0:T(8,128)(2,1)S(1)}, u32[]{:S(2)}, u32[]{:S(2)}) collective-permute-start(bf16[32,4096]{1,0:T(8,128)(2,1)S(1)} %get-tuple-element.21), channel_id=1, source_target_pairs={{0,16},{16,0},{1,17},{17,1},{2,18},{18,2},{3,19},{19,3},{4,20},{20... | collective-permute-start | bytes 786440 | tf_op jit(solution)/shard_map/ppermute | solution.py:185
  47.9 10.9 %collective-permute-start.15 = (bf16[32,4096]{1,0:T(8,128)(2,1)S(1)}, bf16[32,4096]{1,0:T(8,128)(2,1)S(1)}, u32[]{:S(2)}, u32[]{:S(2)}) collective-permute-start(bf16[32,4096]{1,0:T(8,128)(2,1)S(1)} %get-tuple-element.20), channel_id=1, source_target_pairs={{0,16},{16,0},{1,17},{17,1},{2,18},{18,2},{3,19},{19,3},{4,20},{20... | collective-permute-start | bytes 786440 | tf_op jit(solution)/shard_map/ppermute | solution.py:185
  49.4 6.5 %collective-permute-start.11 = (bf16[16,2048]{1,0:T(8,128)(2,1)S(1)}, bf16[16,2048]{1,0:T(8,128)(2,1)S(1)}, u32[]{:S(2)}, u32[]{:S(2)}) collective-permute-start(bf16[16,2048]{1,0:T(8,128)(2,1)S(1)} %slice.151), channel_id=1, source_target_pairs={{0,8},{2,10},{4,12},{6,14},{8,0},{10,2},{12,4},{14,6},{1,9},{3,11}... | collective-permute-start | bytes 196616 | tf_op jit(solution)/shard_map/ppermute | solution.py:185
  55.9 1.3 %collective-permute-start.12 = (bf16[8,2048]{1,0:T(8,128)(2,1)S(1)}, bf16[8,2048]{1,0:T(8,128)(2,1)S(1)}, u32[]{:S(2)}, u32[]{:S(2)}) collective-permute-start(bf16[8,2048]{1,0:T(8,128)(2,1)S(1)} %get-tuple-element.56), channel_id=1, source_target_pairs={{0,1},{1,0},{2,3},{3,2},{4,5},{5,4},{6,7},{7,6},{8,9},{9,8},{10,11... | collective-permute-start | bytes 98312 | tf_op jit(solution)/shard_map/ppermute | solution.py:185
where the time goes:
time: 62.8 us; the launch traced here: 62.6 us
  starting transfers between devices  26.4 us (42%)
  waiting for transfers between devices  20.5 us (33%)
  matrix products  8.45 us (13%)
  local copies, waits for them, and re-layouts  3.87 us (6%)
  Pallas kernels  2.3 us (4%)
  between operations  1 us (2%)
    ppermute x17, starting transfers between devices, swap(): return lax.ppermute(value, axis, pairs)  26.4 us
    ppermute x17, waiting for transfers between devices, swap(): return lax.ppermute(value, axis, pairs)  20.5 us
    unnamed x24, local copies, waits for them, and re-layouts  3.8 us
    pallas_call x1, Pallas kernels, finish(): pl.pallas_call(finish_kernel, out_shape=tuple((jax.ShapeDtypeStruct(g.sha...  1.59 us
    dot_general x5, matrix products, hidden(): lax.dot_general(rows_cot, down_rows, NT, preferred_element_type=jnp.float32)  1.43 us
  transfers between devices with their start and end apart: 17, of which 9 were waited for; matrix products, arithmetic and copies ran while one was open for 11% of the time, Pallas kernels for 0%

commit v1 on v0

--- a/solution.py
+++ b/solution.py
@@ -12,6 +12,9 @@
 CAP = 8
 FAR = 4
 
+
+FRONT_VMEM = 55000 << 10
+CHUNKS = 4
 
 NT = (((1,), (1,)), ((), ()))
 TN = (((0,), (0,)), ((), ()))
@@ -54,16 +57,16 @@
 def front_kernel(window, mine_ref, ids_hbm, probs_hbm, tokens_hbm, cot_hbm, rows_ref, picker_ref,
                  ids_ref, probs_ref, tokens_ref, cot_ref, sems):
     copies = [
-        pltpu.make_async_copy(source, target, sems.at[index])
-        for index, (source, target) in enumerate(
-            (
-                (ids_hbm, ids_ref),
-                (probs_hbm, probs_ref),
-                (tokens_hbm, tokens_ref),
-                (cot_hbm, cot_ref),
+        pltpu.make_async_copy(ids_hbm, ids_ref, sems.at[0]),
+        pltpu.make_async_copy(probs_hbm, probs_ref, sems.at[1]),
+    ]
+    size = tokens_ref.shape[0] // CHUNKS
+    for source, target in ((tokens_hbm, tokens_ref), (cot_hbm, cot_ref)):
+        for index in range(CHUNKS):
+            part = pl.ds(index * size, size)
+            copies.append(
+                pltpu.make_async_copy(source.at[part], target.at[part], sems.at[len(copies)])
             )
-        )
-    ]
     for copy in copies:
         copy.start()
     mine = mine_ref[0]
@@ -93,10 +96,12 @@
     picker = placed.astype(jnp.bfloat16)
     picker_ref[...] = picker
     prob = jnp.sum(jnp.where(placed, chosen, 0.0), axis=1, keepdims=True)
-    copies[2].wait()
+    for copy in copies[2 : 2 + CHUNKS]:
+        copy.wait()
     rows_in = jnp.dot(picker, tokens_ref[...], preferred_element_type=jnp.float32)
     rows_ref[:, :width] = rows_in.astype(jnp.bfloat16)
-    copies[3].wait()
+    for copy in copies[2 + CHUNKS :]:
+        copy.wait()
     rows_cot = jnp.dot(picker, cot_ref[...], preferred_element_type=jnp.float32)
     rows_ref[:, width:] = (prob * rows_cot).astype(jnp.bfloat16)
 
@@ -119,9 +124,9 @@
             pltpu.VMEM(probs.shape, probs.dtype),
             pltpu.VMEM(tokens.shape, tokens.dtype),
             pltpu.VMEM(cotangent.shape, cotangent.dtype),
-            pltpu.SemaphoreType.DMA((4,)),
+            pltpu.SemaphoreType.DMA((2 + 2 * CHUNKS,)),
         ],
-        compiler_params=pltpu.CompilerParams(vmem_limit_bytes=8 << 20),
+        compiler_params=pltpu.CompilerParams(vmem_limit_bytes=FRONT_VMEM),
         name="front",
     )(mine, ids, probs, tokens, cotangent)
 
@@ -140,15 +145,17 @@
         copy.start()
         copies.append(copy)
 
+    units = dgate_ref.shape[1]
+    slopes = jnp.concatenate([dgate_ref[...], dupward_ref[...]], axis=1)
     for index in range(TILES):
         part = pl.ds(index * tile, tile)
         rows_in = rows_ref[:, index * tile : (index + 1) * tile]
         rows_cot = rows_ref[:, width + index * tile : width + (index + 1) * tile]
-        for source, slope, out, hbm, sem in (
-            (gate_ref, dgate_ref, gate_out, gate_hbm, 0),
-            (up_ref, dupward_ref, up_out, up_hbm, 1),
+        both = lax.dot_general(rows_in, slopes, TN, preferred_element_type=jnp.float32)
+        for source, more, out, hbm, sem in (
+            (gate_ref, both[:, :units], gate_out, gate_hbm, 0),
+            (up_ref, both[:, units:], up_out, up_hbm, 1),
         ):
-            more = lax.dot_general(rows_in, slope[...], TN, preferred_element_type=jnp.float32)
             out[part, :] = (source[part, :] + more).astype(jnp.bfloat16)
             send(out.at[part, :], hbm.at[part, :], 3 * index + sem)
         more = lax.dot_general(active_ref[...], rows_cot, TN, preferred_element_type=jnp.float32)
@@ -195,29 +202,43 @@
         held.append(swap(rows[index * CAP : (index + 1) * CAP], "win", index))
 
     rows = {0: join(held)}
-    for mask in (6, 4, 2):
-        rows[mask] = swap(rows[0], "slice", mask)
-    for mask in (0, 2, 6, 4):
-        rows[mask + 1] = swap(rows[mask], "slice", 1)
-
-    def pair(mask):
-        return join([rows[mask], rows[mask ^ FAR]])
-
-    even = join([pair(0), pair(2)])
-    hid_even = hidden(even, *weights)
-    part = part_of(hid_even, *weights[:2])
-    back = part[: 2 * block]
-    part = part[2 * block :].astype(jnp.bfloat16)
-    incoming = [swap(part, "slice", 2)]
-    piece, _ = lax.optimization_barrier((pair(3), part))
-    hid_three = hidden(piece, *weights)
-    part = part_of(hid_three, *weights[:2]).astype(jnp.bfloat16)
-    incoming.append(swap(part, "slice", 3))
-    piece, _ = lax.optimization_barrier((pair(1), part))
-    hid_one = hidden(piece, *weights)
-    part = part_of(hid_one, *weights[:2]).astype(jnp.bfloat16)
-    incoming.append(swap(part, "slice", 1))
-    last = part
+
+    def pair(*masks):
+        return join([rows[mask] for mask in masks])
+
+    def bring(value, mask, *targets):
+        received = swap(value, "slice", mask)
+        for index, target in enumerate(targets):
+            rows[target] = received[index * block : (index + 1) * block]
+
+    bring(rows[0], 4, 4)
+    bring(rows[0], 2, 2)
+    bring(rows[0], 1, 1)
+    bring(rows[4], 2, 6)
+    bring(pair(2, 4), 1, 3, 5)
+    bring(rows[6], 1, 7)
+
+    hids, parts = {}, {}
+
+    def turn(*masks):
+        hid = hidden(pair(*masks), *weights)
+        part = part_of(hid, *weights[:2])
+        for index, mask in enumerate(masks):
+            span = slice(index * block, (index + 1) * block)
+            hids[mask] = [item[span] for item in hid]
+            parts[mask] = part[span]
+
+    def give(mask):
+        value = join([parts[mask], parts[mask ^ 4]]).astype(jnp.bfloat16)
+        return swap(value, "slice", mask)
+
+    turn(0)
+    turn(2, 4)
+    back = lax.optimization_barrier(join([parts[0], parts[4]]))
+    turn(6, 1)
+    turn(3, 5, 7)
+    incoming = [give(mask) for mask in (2, 3, 1)]
+    last = parts[7]
     for part in incoming:
         back = back + part.astype(jnp.float32)
 
@@ -230,11 +251,12 @@
         picker, join(kept), TN, preferred_element_type=jnp.float32
     ).astype(jnp.bfloat16)
 
-    hid = [join(items) for items in zip(hid_even, hid_three, hid_one)]
-    grads = weight_grads(join([even, pair(3), pair(1)]), hid)
+    order = list(rows)
+    hid = [join(items) for items in zip(*(hids[index] for index in order))]
+    grads = weight_grads(pair(*order), hid)
     grads = lax.optimization_barrier(grads)
     for mask in range(1, groups):
-        pieces = [rows[0], join([rows[2], rows[4], rows[6]]), pair(3), pair(1)]
+        pieces = [rows[0], pair(2, 4), pair(1, 6), pair(3, 5, 7)]
         if mask > 1:
             pieces, grads = lax.optimization_barrier((pieces, grads))
         theirs = [swap(piece, "dp", mask) for piece in pieces]
@@ -242,12 +264,13 @@
         early = join(early)
         more = weight_grads(early, hidden(early, *weights))
         grads = tuple(a + b for a, b in zip(grads, more))
-        late, _ = lax.optimization_barrier((theirs[-1], grad_input))
+        late = theirs[-1]
         hid = hidden(late, *weights)
         if mask < groups - 1:
             more = weight_grads(late, hid)
             grads = tuple(a + b for a, b in zip(grads, more))
-    grads = finish(grads, late, hid)
+        else:
+            grads = finish(grads, late, hid)
     return (grad_input,) + tuple(g[None] for g in grads)
 
 

time: 62.8 us -> 55.5 us (0.88)
  starting transfers between devices: 26.4 us -> 22.2 us
  local copies, waits for them, and re-layouts: 3.87 us -> 1.13 us
  waiting for transfers between devices: 20.5 us -> 18 us
  matrix products: 8.45 us -> 9.62 us
  Pallas kernels: 2.3 us -> 3.16 us
    ppermute x17 -> x16, starting transfers between devices: 26.4 us -> 22.2 us  [swap(): return lax.ppermute(value, axis, pairs)]
    unnamed x24 -> x30, local copies, waits for them, and re-layouts: 3.8 us -> 1 us
    ppermute x17 -> x16, waiting for transfers between devices: 20.5 us -> 18 us  [swap(): return lax.ppermute(value, axis, pairs)]
    pallas_call x1, Pallas kernels: 0.7 us -> 1.56 us  [front(): pl.pallas_call(functools.partial(front_kernel, window), out_shape=(jax.Sh...]
    dot_general x5 -> x6, matrix products: 1.43 us -> 1.7 us  [hidden(): lax.dot_general(rows_cot, down_rows, NT, preferred_element_type=jnp.float32)]
    dot_general x5 -> x6, matrix products: 1.08 us -> 1.32 us  [hidden(): gate_pre = jnp.dot(rows_in, gate_rows, preferred_element_type=jnp.float32)]
    dot_general x5 -> x6, matrix products: 1.14 us -> 1.29 us  [hidden(): upward = jnp.dot(rows_in, up_rows, preferred_element_type=jnp.float32)]
  transfers between devices with their start and end apart: 17 -> 16, of which waited for: 9 -> 9; matrix products, arithmetic and copies ran while one was open for 11% -> 17% of each run, Pallas kernels for 0% -> 0%
where the time goes in v1:
time: 55.5 us; the launch traced here: 55.3 us
  starting transfers between devices  22.2 us (40%)
  waiting for transfers between devices  18 us (32%)
  matrix products  9.62 us (17%)
  Pallas kernels  3.16 us (6%)
  local copies, waits for them, and re-layouts  1.13 us (2%)
  between operations  1.06 us (2%)
    ppermute x16, starting transfers between devices, swap(): return lax.ppermute(value, axis, pairs)  22.2 us
    ppermute x16, waiting for transfers between devices, swap(): return lax.ppermute(value, axis, pairs)  18 us
    dot_general x6, matrix products, hidden(): lax.dot_general(rows_cot, down_rows, NT, preferred_element_type=jnp.float32)  1.7 us
    pallas_call x1, Pallas kernels, finish(): pl.pallas_call(finish_kernel, out_shape=tuple((jax.ShapeDtypeStruct(g.sha...  1.6 us
    pallas_call x1, Pallas kernels, front(): pl.pallas_call(functools.partial(front_kernel, window), out_shape=(jax.Sh...  1.56 us
    dot_general x6, matrix products, hidden(): gate_pre = jnp.dot(rows_in, gate_rows, preferred_element_type=jnp.float32)  1.32 us
    dot_general x6, matrix products, hidden(): upward = jnp.dot(rows_in, up_rows, preferred_element_type=jnp.float32)  1.29 us
    dot_general x4, matrix products, part_of(): lax.dot_general(hid[2], up_rows, NT, preferred_element_type=jnp.float32)  1.12 us
  transfers between devices with their start and end apart: 16, of which 9 were waited for; matrix products, arithmetic and copies ran while one was open for 17% of the time, Pallas kernels for 0%

profile of v1, /device:TPU:0, one launch (start us, length us, event | category | flops | bytes accessed | tf_op | source)
XLA Modules:
  0.0 55.3 jit_solution(2148233552045181229)
XLA Ops:
  0.7 0.7 %copy-done.2 = f32[128,8]{0,1:T(8,128)S(1)} copy-done((f32[128,8]{0,1:T(8,128)S(1)}, f32[128,8]{0,1:T(8,128)}, u32[]{:S(2)}) %copy-start.2) | copy-done | bytes 4120
  1.4 1.6 %front.1 = (bf16[16,4096]{1,0:T(8,128)(2,1)S(1)}, bf16[16,128]{1,0:T(8,128)(2,1)S(1)}) custom-call(s32[1]{0:T(128)} %bitcast.mine_ref, s32[8,128]{1,0:T(8,128)S(1)} %bitcast.83, f32[8,128]{1,0:T(8,128)S(1)} %bitcast.84, bf16[128,2048]{1,0:T(8,128)(2,1)} %tokens_hbm.1, bf16[128,2048]{1,0:T(8,128)(2,1)} %cot_hbm.1), custom_call_target="tpu_custom_call" | custom-call | tf_op jit(solution)/shard_map/front/pallas_call | solution.py:114
  3.6 0.9 %collective-permute-done = bf16[8,4096]{1,0:T(8,128)(2,1)S(1)} collective-permute-done((bf16[8,4096]{1,0:T(8,128)(2,1)S(1)}, bf16[8,4096]{1,0:T(8,128)(2,1)S(1)}, u32[]{:S(2)}, u32[]{:S(2)}) %collective-permute-start) | collective-permute-done | bytes 65568 | tf_op jit(solution)/shard_map/ppermute | solution.py:192
  4.5 4.0 %collective-permute-start.2 = (bf16[16,4096]{1,0:T(8,128)(2,1)S(1)}, bf16[16,4096]{1,0:T(8,128)(2,1)S(1)}, u32[]{:S(2)}, u32[]{:S(2)}) collective-permute-start(bf16[16,4096]{1,0:T(8,128)(2,1)S(1)} %pad_maximum_fusion.2), channel_id=1, source_target_pairs={{0,8},{2,10},{4,12},{6,14},{8,0},{10,2},{12,4},{14,6},{1,9},{3,11}... | collective-permute-start | bytes 393224 | tf_op jit(solution)/shard_map/ppermute | solution.py:192
  8.5 1.6 %collective-permute-start.1 = (bf16[16,4096]{1,0:T(8,128)(2,1)S(1)}, bf16[16,4096]{1,0:T(8,128)(2,1)S(1)}, u32[]{:S(2)}, u32[]{:S(2)}) collective-permute-start(bf16[16,4096]{1,0:T(8,128)(2,1)S(1)} %pad_maximum_fusion.2), channel_id=1, source_target_pairs={{0,4},{2,6},{4,0},{6,2},{8,12},{10,14},{12,8},{14,10},{1,5},{3,7},... | collective-permute-start | bytes 393224 | tf_op jit(solution)/shard_map/ppermute | solution.py:192
  10.1 1.5 %collective-permute-start.4 = (bf16[16,4096]{1,0:T(8,128)(2,1)S(1)}, bf16[16,4096]{1,0:T(8,128)(2,1)S(1)}, u32[]{:S(2)}, u32[]{:S(2)}) collective-permute-start(bf16[16,4096]{1,0:T(8,128)(2,1)S(1)} %pad_maximum_fusion.2), channel_id=1, source_target_pairs={{0,2},{2,0},{4,6},{6,4},{8,10},{10,8},{12,14},{14,12},{1,3},{3,1},... | collective-permute-start | bytes 393224 | tf_op jit(solution)/shard_map/ppermute | solution.py:192
  11.6 1.5 %collective-permute-start.12 = (bf16[16,4096]{1,0:T(8,128)(2,1)S(1)}, bf16[16,4096]{1,0:T(8,128)(2,1)S(1)}, u32[]{:S(2)}, u32[]{:S(2)}) collective-permute-start(bf16[16,4096]{1,0:T(8,128)(2,1)S(1)} %pad_maximum_fusion.2), channel_id=1, source_target_pairs={{0,16},{16,0},{1,17},{17,1},{2,18},{18,2},{3,19},{19,3},{4,20},{20... | collective-permute-start | bytes 393224 | tf_op jit(solution)/shard_map/ppermute | solution.py:192
  14.2 1.0 %collective-permute-done.2 = bf16[16,4096]{1,0:T(8,128)(2,1)S(1)} collective-permute-done((bf16[16,4096]{1,0:T(8,128)(2,1)S(1)}, bf16[16,4096]{1,0:T(8,128)(2,1)S(1)}, u32[]{:S(2)}, u32[]{:S(2)}) %collective-permute-start.2) | collective-permute-done | bytes 131104 | tf_op jit(solution)/shard_map/ppermute | solution.py:192
  15.5 1.6 %collective-permute-start.6 = (bf16[32,4096]{1,0:T(8,128)(2,1)S(1)}, bf16[32,4096]{1,0:T(8,128)(2,1)S(1)}, u32[]{:S(2)}, u32[]{:S(2)}) collective-permute-start(bf16[32,4096]{1,0:T(8,128)(2,1)S(1)} %constant_dynamic-update-slice_fusion), channel_id=1, source_target_pairs={{0,2},{2,0},{4,6},{6,4},{8,10},{10,8},{12,14},{14,12},{1,3},{3,1},... | collective-permute-start | bytes 786440 | tf_op jit(solution)/shard_map/ppermute | solution.py:192
  17.1 1.5 %collective-permute-start.13 = (bf16[32,4096]{1,0:T(8,128)(2,1)S(1)}, bf16[32,4096]{1,0:T(8,128)(2,1)S(1)}, u32[]{:S(2)}, u32[]{:S(2)}) collective-permute-start(bf16[32,4096]{1,0:T(8,128)(2,1)S(1)} %constant_dynamic-update-slice_fusion), channel_id=1, source_target_pairs={{0,16},{16,0},{1,17},{17,1},{2,18},{18,2},{3,19},{19,3},{4,20},{20... | collective-permute-start | bytes 786440 | tf_op jit(solution)/shard_map/ppermute | solution.py:192
  20.0 1.5 %collective-permute-start.3 = (bf16[16,4096]{1,0:T(8,128)(2,1)S(1)}, bf16[16,4096]{1,0:T(8,128)(2,1)S(1)}, u32[]{:S(2)}, u32[]{:S(2)}) collective-permute-start(bf16[16,4096]{1,0:T(8,128)(2,1)S(1)} %collective-permute-done.2), channel_id=1, source_target_pairs={{0,4},{2,6},{4,0},{6,2},{8,12},{10,14},{12,8},{14,10},{1,5},{3,7},... | collective-permute-start | bytes 393224 | tf_op jit(solution)/shard_map/ppermute | solution.py:192
  21.5 3.5 %collective-permute-done.3 = bf16[16,4096]{1,0:T(8,128)(2,1)S(1)} collective-permute-done((bf16[16,4096]{1,0:T(8,128)(2,1)S(1)}, bf16[16,4096]{1,0:T(8,128)(2,1)S(1)}, u32[]{:S(2)}, u32[]{:S(2)}) %collective-permute-start.3) | collective-permute-done | bytes 131104 | tf_op jit(solution)/shard_map/ppermute | solution.py:192
  25.6 0.6 %collective-permute-start.14 = (bf16[32,4096]{1,0:T(8,128)(2,1)S(1)}, bf16[32,4096]{1,0:T(8,128)(2,1)S(1)}, u32[]{:S(2)}, u32[]{:S(2)}) collective-permute-start(bf16[32,4096]{1,0:T(8,128)(2,1)S(1)} %pad_maximum_fusion.1), channel_id=1, source_target_pairs={{0,16},{16,0},{1,17},{17,1},{2,18},{18,2},{3,19},{19,3},{4,20},{20... | collective-permute-start | bytes 786440 | tf_op jit(solution)/shard_map/ppermute | solution.py:192
  27.0 1.5 %collective-permute-start.5 = (bf16[32,2048]{1,0:T(8,128)(2,1)S(1)}, bf16[32,2048]{1,0:T(8,128)(2,1)S(1)}, u32[]{:S(2)}, u32[]{:S(2)}) collective-permute-start(bf16[32,2048]{1,0:T(8,128)(2,1)S(1)} %pad_maximum_fusion.3), channel_id=1, source_target_pairs={{0,4},{2,6},{4,0},{6,2},{8,12},{10,14},{12,8},{14,10},{1,5},{3,7},... | collective-permute-start | bytes 393224 | tf_op jit(solution)/shard_map/ppermute | solution.py:192
  29.1 4.4 %collective-permute-done.7 = bf16[16,4096]{1,0:T(8,128)(2,1)S(1)} collective-permute-done((bf16[16,4096]{1,0:T(8,128)(2,1)S(1)}, bf16[16,4096]{1,0:T(8,128)(2,1)S(1)}, u32[]{:S(2)}, u32[]{:S(2)}) %collective-permute-start.7) | collective-permute-done | bytes 131104 | tf_op jit(solution)/shard_map/ppermute | solution.py:192
  33.5 1.6 %collective-permute-start.15 = (bf16[48,4096]{1,0:T(8,128)(2,1)S(1)}, bf16[48,4096]{1,0:T(8,128)(2,1)S(1)}, u32[]{:S(2)}, u32[]{:S(2)}) collective-permute-start(bf16[48,4096]{1,0:T(8,128)(2,1)S(1)} %get-tuple-element.40), channel_id=1, source_target_pairs={{0,16},{16,0},{1,17},{17,1},{2,18},{18,2},{3,19},{19,3},{4,20},{20... | collective-permute-start | bytes 1179656 | tf_op jit(solution)/shard_map/ppermute | solution.py:192
  38.1 1.5 %collective-permute-start.9 = (bf16[32,2048]{1,0:T(8,128)(2,1)S(1)}, bf16[32,2048]{1,0:T(8,128)(2,1)S(1)}, u32[]{:S(2)}, u32[]{:S(2)}) collective-permute-start(bf16[32,2048]{1,0:T(8,128)(2,1)S(1)} %pad_maximum_fusion.5), channel_id=1, source_target_pairs={{0,2},{2,0},{4,6},{6,4},{8,10},{10,8},{12,14},{14,12},{1,3},{3,1},... | collective-permute-start | bytes 393224 | tf_op jit(solution)/shard_map/ppermute | solution.py:192
  40.9 2.7 %collective-permute-done.8 = bf16[32,2048]{1,0:T(8,128)(2,1)S(1)} collective-permute-done((bf16[32,2048]{1,0:T(8,128)(2,1)S(1)}, bf16[32,2048]{1,0:T(8,128)(2,1)S(1)}, u32[]{:S(2)}, u32[]{:S(2)}) %collective-permute-start.8) | collective-permute-done | bytes 131104 | tf_op jit(solution)/shard_map/ppermute | solution.py:192
  43.6 0.9 %collective-permute-done.9 = bf16[32,2048]{1,0:T(8,128)(2,1)S(1)} collective-permute-done((bf16[32,2048]{1,0:T(8,128)(2,1)S(1)}, bf16[32,2048]{1,0:T(8,128)(2,1)S(1)}, u32[]{:S(2)}, u32[]{:S(2)}) %collective-permute-start.9) | collective-permute-done | bytes 131104 | tf_op jit(solution)/shard_map/ppermute | solution.py:192
  44.6 2.1 %collective-permute-start.10 = (bf16[16,2048]{1,0:T(8,128)(2,1)S(1)}, bf16[16,2048]{1,0:T(8,128)(2,1)S(1)}, u32[]{:S(2)}, u32[]{:S(2)}) collective-permute-start(bf16[16,2048]{1,0:T(8,128)(2,1)S(1)} %slice.298), channel_id=1, source_target_pairs={{0,8},{2,10},{4,12},{6,14},{8,0},{10,2},{12,4},{14,6},{1,9},{3,11}... | collective-permute-start | bytes 196616 | tf_op jit(solution)/shard_map/ppermute | solution.py:192
  47.0 3.5 %collective-permute-done.10 = bf16[16,2048]{1,0:T(8,128)(2,1)S(1)} collective-permute-done((bf16[16,2048]{1,0:T(8,128)(2,1)S(1)}, bf16[16,2048]{1,0:T(8,128)(2,1)S(1)}, u32[]{:S(2)}, u32[]{:S(2)}) %collective-permute-start.10) | collective-permute-done | bytes 65568 | tf_op jit(solution)/shard_map/ppermute | solution.py:192
  51.0 0.9 %collective-permute-done.11 = bf16[8,2048]{1,0:T(8,128)(2,1)S(1)} collective-permute-done((bf16[8,2048]{1,0:T(8,128)(2,1)S(1)}, bf16[8,2048]{1,0:T(8,128)(2,1)S(1)}, u32[]{:S(2)}, u32[]{:S(2)}) %collective-permute-start.11) | collective-permute-done | bytes 32800 | tf_op jit(solution)/shard_map/ppermute | solution.py:192
  51.8 1.1 %convolution_convert_fusion = bf16[128,2048]{1,0:T(8,128)(2,1)} fusion(bf16[16,128]{1,0:T(8,128)(2,1)S(1)} %get-tuple-element.15, bf16[8,2048]{1,0:T(8,128)(2,1)S(1)} %collective-permute-done.11, bf16[8,2048]{1,0:T(8,128)(2,1)S(1)} %get-tuple-element.50), kind=kOutput, calls=%fused_computation.3 | convolution fusion | flops 8781824 | bytes 593920 | tf_op jit(solution)/shard_map/dot_general | solution.py:250
  53.7 1.6 %finish.1 = (bf16[2048,128]{1,0:T(8,128)(2,1)}, bf16[2048,128]{1,0:T(8,128)(2,1)}, bf16[128,2048]{1,0:T(8,128)(2,1)}) custom-call(f32[2048,128]{1,0:T(8,128)S(1)} %convolution_add_fusion.2.gate_ref, f32[2048,128]{1,0:T(8,128)S(1)} %convolution_add_fusion.1.up_ref, f32[128,2048]{1,0:T(8,128)S(1)} %convolution_add_fusion.down_ref, ...), custom_call_target="tpu_custom_call" | custom-call | tf_op jit(solution)/shard_map/finish/pallas_call | solution.py:171
  (91 shorter events, 11.0 us)
Async XLA Ops:
  0.6 12.9 %copy-start = (bf16[1,2048,128]{2,1,0:T(8,128)(2,1)S(1)}, bf16[1,2048,128]{2,1,0:T(8,128)(2,1)}, u32[]{:S(2)}) copy-start(bf16[1,2048,128]{2,1,0:T(8,128)(2,1)} %param.11) | copy-start | bytes 1572868
  0.6 0.7 %copy-start.2 = (f32[128,8]{0,1:T(8,128)S(1)}, f32[128,8]{0,1:T(8,128)}, u32[]{:S(2)}) copy-start(f32[128,8]{0,1:T(8,128)} %param.10) | copy-start | bytes 12292
  0.7 0.8 %copy-start.1 = (s32[128,8]{0,1:T(8,128)S(1)}, s32[128,8]{0,1:T(8,128)}, u32[]{:S(2)}) copy-start(s32[128,8]{0,1:T(8,128)} %param.9) | copy-start | bytes 12292
  3.0 10.1 %copy-start.3 = (bf16[1,2048,128]{2,1,0:T(8,128)(2,1)S(1)}, bf16[1,2048,128]{2,1,0:T(8,128)(2,1)}, u32[]{:S(2)}) copy-start(bf16[1,2048,128]{2,1,0:T(8,128)(2,1)} %param.12) | copy-start | bytes 1572868
  3.0 10.2 %copy-start.4 = (bf16[1,128,2048]{2,1,0:T(8,128)(2,1)S(1)}, bf16[1,128,2048]{2,1,0:T(8,128)(2,1)}, u32[]{:S(2)}) copy-start(bf16[1,128,2048]{2,1,0:T(8,128)(2,1)} %param.13) | copy-start | bytes 1572868
  3.0 1.5 %collective-permute-start = (bf16[8,4096]{1,0:T(8,128)(2,1)S(1)}, bf16[8,4096]{1,0:T(8,128)(2,1)S(1)}, u32[]{:S(2)}, u32[]{:S(2)}) collective-permute-start(bf16[8,4096]{1,0:T(8,128)(2,1)S(1)} %get-tuple-element.46), channel_id=1, source_target_pairs={{0,1},{1,0},{2,3},{3,2},{4,5},{5,4},{6,7},{7,6},{8,9},{9,8},{10,11... | collective-permute-start | bytes 196616 | tf_op jit(solution)/shard_map/ppermute | solution.py:192
  4.5 10.7 %collective-permute-start.2 = (bf16[16,4096]{1,0:T(8,128)(2,1)S(1)}, bf16[16,4096]{1,0:T(8,128)(2,1)S(1)}, u32[]{:S(2)}, u32[]{:S(2)}) collective-permute-start(bf16[16,4096]{1,0:T(8,128)(2,1)S(1)} %pad_maximum_fusion.2), channel_id=1, source_target_pairs={{0,8},{2,10},{4,12},{6,14},{8,0},{10,2},{12,4},{14,6},{1,9},{3,11}... | collective-permute-start | bytes 393224 | tf_op jit(solution)/shard_map/ppermute | solution.py:192
  8.5 6.9 %collective-permute-start.1 = (bf16[16,4096]{1,0:T(8,128)(2,1)S(1)}, bf16[16,4096]{1,0:T(8,128)(2,1)S(1)}, u32[]{:S(2)}, u32[]{:S(2)}) collective-permute-start(bf16[16,4096]{1,0:T(8,128)(2,1)S(1)} %pad_maximum_fusion.2), channel_id=1, source_target_pairs={{0,4},{2,6},{4,0},{6,2},{8,12},{10,14},{12,8},{14,10},{1,5},{3,7},... | collective-permute-start | bytes 393224 | tf_op jit(solution)/shard_map/ppermute | solution.py:192
  10.1 11.4 %collective-permute-start.4 = (bf16[16,4096]{1,0:T(8,128)(2,1)S(1)}, bf16[16,4096]{1,0:T(8,128)(2,1)S(1)}, u32[]{:S(2)}, u32[]{:S(2)}) collective-permute-start(bf16[16,4096]{1,0:T(8,128)(2,1)S(1)} %pad_maximum_fusion.2), channel_id=1, source_target_pairs={{0,2},{2,0},{4,6},{6,4},{8,10},{10,8},{12,14},{14,12},{1,3},{3,1},... | collective-permute-start | bytes 393224 | tf_op jit(solution)/shard_map/ppermute | solution.py:192
  11.6 25.9 %collective-permute-start.12 = (bf16[16,4096]{1,0:T(8,128)(2,1)S(1)}, bf16[16,4096]{1,0:T(8,128)(2,1)S(1)}, u32[]{:S(2)}, u32[]{:S(2)}) collective-permute-start(bf16[16,4096]{1,0:T(8,128)(2,1)S(1)} %pad_maximum_fusion.2), channel_id=1, source_target_pairs={{0,16},{16,0},{1,17},{17,1},{2,18},{18,2},{3,19},{19,3},{4,20},{20... | collective-permute-start | bytes 393224 | tf_op jit(solution)/shard_map/ppermute | solution.py:192
  15.5 13.1 %collective-permute-start.6 = (bf16[32,4096]{1,0:T(8,128)(2,1)S(1)}, bf16[32,4096]{1,0:T(8,128)(2,1)S(1)}, u32[]{:S(2)}, u32[]{:S(2)}) collective-permute-start(bf16[32,4096]{1,0:T(8,128)(2,1)S(1)} %constant_dynamic-update-slice_fusion), channel_id=1, source_target_pairs={{0,2},{2,0},{4,6},{6,4},{8,10},{10,8},{12,14},{14,12},{1,3},{3,1},... | collective-permute-start | bytes 786440 | tf_op jit(solution)/shard_map/ppermute | solution.py:192
  17.1 21.0 %collective-permute-start.13 = (bf16[32,4096]{1,0:T(8,128)(2,1)S(1)}, bf16[32,4096]{1,0:T(8,128)(2,1)S(1)}, u32[]{:S(2)}, u32[]{:S(2)}) collective-permute-start(bf16[32,4096]{1,0:T(8,128)(2,1)S(1)} %constant_dynamic-update-slice_fusion), channel_id=1, source_target_pairs={{0,16},{16,0},{1,17},{17,1},{2,18},{18,2},{3,19},{19,3},{4,20},{20... | collective-permute-start | bytes 786440 | tf_op jit(solution)/shard_map/ppermute | solution.py:192
  20.0 5.0 %collective-permute-start.3 = (bf16[16,4096]{1,0:T(8,128)(2,1)S(1)}, bf16[16,4096]{1,0:T(8,128)(2,1)S(1)}, u32[]{:S(2)}, u32[]{:S(2)}) collective-permute-start(bf16[16,4096]{1,0:T(8,128)(2,1)S(1)} %collective-permute-done.2), channel_id=1, source_target_pairs={{0,4},{2,6},{4,0},{6,2},{8,12},{10,14},{12,8},{14,10},{1,5},{3,7},... | collective-permute-start | bytes 393224 | tf_op jit(solution)/shard_map/ppermute | solution.py:192
  25.6 14.1 %collective-permute-start.14 = (bf16[32,4096]{1,0:T(8,128)(2,1)S(1)}, bf16[32,4096]{1,0:T(8,128)(2,1)S(1)}, u32[]{:S(2)}, u32[]{:S(2)}) collective-permute-start(bf16[32,4096]{1,0:T(8,128)(2,1)S(1)} %pad_maximum_fusion.1), channel_id=1, source_target_pairs={{0,16},{16,0},{1,17},{17,1},{2,18},{18,2},{3,19},{19,3},{4,20},{20... | collective-permute-start | bytes 786440 | tf_op jit(solution)/shard_map/ppermute | solution.py:192
  27.0 13.9 %collective-permute-start.5 = (bf16[32,2048]{1,0:T(8,128)(2,1)S(1)}, bf16[32,2048]{1,0:T(8,128)(2,1)S(1)}, u32[]{:S(2)}, u32[]{:S(2)}) collective-permute-start(bf16[32,2048]{1,0:T(8,128)(2,1)S(1)} %pad_maximum_fusion.3), channel_id=1, source_target_pairs={{0,4},{2,6},{4,0},{6,2},{8,12},{10,14},{12,8},{14,10},{1,5},{3,7},... | collective-permute-start | bytes 393224 | tf_op jit(solution)/shard_map/ppermute | solution.py:192
  28.6 5.0 %collective-permute-start.7 = (bf16[16,4096]{1,0:T(8,128)(2,1)S(1)}, bf16[16,4096]{1,0:T(8,128)(2,1)S(1)}, u32[]{:S(2)}, u32[]{:S(2)}) collective-permute-start(bf16[16,4096]{1,0:T(8,128)(2,1)S(1)} %collective-permute-done.3), channel_id=1, source_target_pairs={{0,2},{2,0},{4,6},{6,4},{8,10},{10,8},{12,14},{14,12},{1,3},{3,1},... | collective-permute-start | bytes 393224 | tf_op jit(solution)/shard_map/ppermute | solution.py:192
  33.5 19.4 %collective-permute-start.15 = (bf16[48,4096]{1,0:T(8,128)(2,1)S(1)}, bf16[48,4096]{1,0:T(8,128)(2,1)S(1)}, u32[]{:S(2)}, u32[]{:S(2)}) collective-permute-start(bf16[48,4096]{1,0:T(8,128)(2,1)S(1)} %get-tuple-element.40), channel_id=1, source_target_pairs={{0,16},{16,0},{1,17},{17,1},{2,18},{18,2},{3,19},{19,3},{4,20},{20... | collective-permute-start | bytes 1179656 | tf_op jit(solution)/shard_map/ppermute | solution.py:192
  37.5 6.0 %collective-permute-start.8 = (bf16[32,2048]{1,0:T(8,128)(2,1)S(1)}, bf16[32,2048]{1,0:T(8,128)(2,1)S(1)}, u32[]{:S(2)}, u32[]{:S(2)}) collective-permute-start(bf16[32,2048]{1,0:T(8,128)(2,1)S(1)} %pad_maximum_fusion.4), channel_id=1, source_target_pairs={{0,6},{2,4},{4,2},{6,0},{8,14},{10,12},{12,10},{14,8},{1,7},{3,5},... | collective-permute-start | bytes 393224 | tf_op jit(solution)/shard_map/ppermute | solution.py:192
  38.1 6.4 %collective-permute-start.9 = (bf16[32,2048]{1,0:T(8,128)(2,1)S(1)}, bf16[32,2048]{1,0:T(8,128)(2,1)S(1)}, u32[]{:S(2)}, u32[]{:S(2)}) collective-permute-start(bf16[32,2048]{1,0:T(8,128)(2,1)S(1)} %pad_maximum_fusion.5), channel_id=1, source_target_pairs={{0,2},{2,0},{4,6},{6,4},{8,10},{10,8},{12,14},{14,12},{1,3},{3,1},... | collective-permute-start | bytes 393224 | tf_op jit(solution)/shard_map/ppermute | solution.py:192
  44.6 5.9 %collective-permute-start.10 = (bf16[16,2048]{1,0:T(8,128)(2,1)S(1)}, bf16[16,2048]{1,0:T(8,128)(2,1)S(1)}, u32[]{:S(2)}, u32[]{:S(2)}) collective-permute-start(bf16[16,2048]{1,0:T(8,128)(2,1)S(1)} %slice.298), channel_id=1, source_target_pairs={{0,8},{2,10},{4,12},{6,14},{8,0},{10,2},{12,4},{14,6},{1,9},{3,11}... | collective-permute-start | bytes 196616 | tf_op jit(solution)/shard_map/ppermute | solution.py:192
  50.6 1.3 %collective-permute-start.11 = (bf16[8,2048]{1,0:T(8,128)(2,1)S(1)}, bf16[8,2048]{1,0:T(8,128)(2,1)S(1)}, u32[]{:S(2)}, u32[]{:S(2)}) collective-permute-start(bf16[8,2048]{1,0:T(8,128)(2,1)S(1)} %get-tuple-element.51), channel_id=1, source_target_pairs={{0,1},{1,0},{2,3},{3,2},{4,5},{5,4},{6,7},{7,6},{8,9},{9,8},{10,11... | collective-permute-start | bytes 98312 | tf_op jit(solution)/shard_map/ppermute | solution.py:192

commit v2 on v1

--- a/solution.py
+++ b/solution.py
@@ -195,13 +195,24 @@
         return jnp.concatenate(items, axis=0)
 
     rows, picker = front(
-        mine.astype(jnp.int32)[None], expert_ids.T, gate_probs.T, tokens, cotangent, window
-    )
-    held = [rows[:CAP]]
+        mine.astype(jnp.int32)[None],
+        pltpu.with_memory_space_constraint(expert_ids.T, pltpu.HBM),
+        pltpu.with_memory_space_constraint(gate_probs.T, pltpu.HBM),
+        tokens, cotangent, window
+    )
+    split = [rows[index * CAP : (index + 1) * CAP] for index in range(window)]
+    near = [split[0]]
     for index in range(1, window):
-        held.append(swap(rows[index * CAP : (index + 1) * CAP], "win", index))
-
-    rows = {0: join(held)}
+        near.append(swap(split[index], "win", index))
+    far = []
+    for index in range(window):
+        pairs = []
+        for s in range(SLICES):
+            for e in range(window):
+                pairs.append((s * window + e, (s ^ FAR) * window + (e ^ index)))
+        far.append(lax.ppermute(split[index], ("slice", "win"), pairs))
+
+    rows = {0: join(near), FAR: join(far)}
 
     def pair(*masks):
         return join([rows[mask] for mask in masks])
@@ -211,7 +222,6 @@
         for index, target in enumerate(targets):
             rows[target] = received[index * block : (index + 1) * block]
 
-    bring(rows[0], 4, 4)
     bring(rows[0], 2, 2)
     bring(rows[0], 1, 1)
     bring(rows[4], 2, 6)
@@ -253,8 +263,7 @@
 
     order = list(rows)
     hid = [join(items) for items in zip(*(hids[index] for index in order))]
-    grads = weight_grads(pair(*order), hid)
-    grads = lax.optimization_barrier(grads)
+    base, grads = pair(*order), None
     for mask in range(1, groups):
         pieces = [rows[0], pair(2, 4), pair(1, 6), pair(3, 5, 7)]
         if mask > 1:
@@ -262,15 +271,19 @@
         theirs = [swap(piece, "dp", mask) for piece in pieces]
         early, _ = lax.optimization_barrier((theirs[:-1], last))
         early = join(early)
-        more = weight_grads(early, hidden(early, *weights))
-        grads = tuple(a + b for a, b in zip(grads, more))
+        more = hidden(early, *weights)
+        if grads is None:
+            early = join([base, early])
+            more = [join(items) for items in zip(hid, more)]
+        more = weight_grads(early, more)
+        grads = more if grads is None else tuple(a + b for a, b in zip(grads, more))
         late = theirs[-1]
-        hid = hidden(late, *weights)
+        more = hidden(late, *weights)
         if mask < groups - 1:
-            more = weight_grads(late, hid)
+            more = weight_grads(late, more)
             grads = tuple(a + b for a, b in zip(grads, more))
-        else:
-            grads = finish(grads, late, hid)
+        if mask == groups - 1:
+            grads = finish(grads, late, more)
     return (grad_input,) + tuple(g[None] for g in grads)
 
 

time: 55.5 us -> 54.6 us (0.984)
  starting transfers between devices: 22.2 us -> 25.5 us
  waiting for transfers between devices: 18 us -> 15 us
  matrix products: 9.62 us -> 8.91 us
  local copies, waits for them, and re-layouts: 1.13 us -> 0.46 us
    ppermute x16 -> x15, waiting for transfers between devices: 18 us -> 13.2 us  [swap(): return lax.ppermute(value, axis, pairs)]
    ppermute x0 -> x2, starting transfers between devices: none -> 3.73 us  [local(): far.append(lax.ppermute(split[index], ('slice', 'win'), pairs))]
    ppermute x0 -> x2, waiting for transfers between devices: none -> 1.84 us  [local(): far.append(lax.ppermute(split[index], ('slice', 'win'), pairs))]
    unnamed x30 -> x29, local copies, waits for them, and re-layouts: 1 us -> 0.34 us
    ppermute x16 -> x15, starting transfers between devices: 22.2 us -> 21.8 us  [swap(): return lax.ppermute(value, axis, pairs)]
  transfers between devices with their start and end apart: 16 -> 17, of which waited for: 9 -> 8; matrix products, arithmetic and copies ran while one was open for 17% -> 16% of each run, Pallas kernels for 0% -> 0%
where the time goes in v2:
time: 54.6 us; the launch traced here: 54.4 us
  starting transfers between devices  25.5 us (47%)
  waiting for transfers between devices  15 us (27%)
  matrix products  8.91 us (16%)
  Pallas kernels  3.31 us (6%)
  between operations  1.05 us (2%)
    ppermute x15, starting transfers between devices, swap(): return lax.ppermute(value, axis, pairs)  21.8 us
    ppermute x15, waiting for transfers between devices, swap(): return lax.ppermute(value, axis, pairs)  13.2 us
    ppermute x2, starting transfers between devices, local(): far.append(lax.ppermute(split[index], ('slice', 'win'), pairs))  3.73 us
    ppermute x2, waiting for transfers between devices, local(): far.append(lax.ppermute(split[index], ('slice', 'win'), pairs))  1.84 us
    dot_general x6, matrix products, hidden(): lax.dot_general(rows_cot, down_rows, NT, preferred_element_type=jnp.float32)  1.72 us
    pallas_call x1, Pallas kernels, front(): pl.pallas_call(functools.partial(front_kernel, window), out_shape=(jax.Sh...  1.71 us
    pallas_call x1, Pallas kernels, finish(): pl.pallas_call(finish_kernel, out_shape=tuple((jax.ShapeDtypeStruct(g.sha...  1.6 us
    dot_general x6, matrix products, hidden(): gate_pre = jnp.dot(rows_in, gate_rows, preferred_element_type=jnp.float32)  1.32 us
  transfers between devices with their start and end apart: 17, of which 8 were waited for; matrix products, arithmetic and copies ran while one was open for 16% of the time, Pallas kernels for 0%

profile of v2, /device:TPU:0, one launch (start us, length us, event | category | flops | bytes accessed | tf_op | source)
XLA Modules:
  0.0 54.4 jit_solution(6850115689457202632)
XLA Ops:
  0.7 1.7 %front.1 = (bf16[16,4096]{1,0:T(8,128)(2,1)S(1)}, bf16[16,128]{1,0:T(8,128)(2,1)S(1)}) custom-call(s32[1]{0:T(128)} %bitcast.mine_ref, s32[8,128]{1,0:T(8,128)} %bitcast.85, f32[8,128]{1,0:T(8,128)} %bitcast.86, bf16[128,2048]{1,0:T(8,128)(2,1)} %tokens_hbm.1, bf16[128,2048]{1,0:T(8,128)(2,1)} %cot_hbm.1), custom_call_target="tpu_custom_call" | custom-call | tf_op jit(solution)/shard_map/front/pallas_call | solution.py:114
  3.0 3.7 %collective-permute-start.3 = (bf16[8,4096]{1,0:T(8,128)(2,1)S(1)}, bf16[8,4096]{1,0:T(8,128)(2,1)S(1)}, u32[]{:S(2)}, u32[]{:S(2)}) collective-permute-start(bf16[8,4096]{1,0:T(8,128)(2,1)S(1)} %get-tuple-element.46), channel_id=1, source_target_pairs={{0,9},{1,8},{2,11},{3,10},{4,13},{5,12},{6,15},{7,14},{8,1},{9,0},... | collective-permute-start | bytes 196616 | tf_op jit(solution)/shard_map/ppermute | solution.py:213
  6.7 1.9 %collective-permute-start.1 = (bf16[16,4096]{1,0:T(8,128)(2,1)S(1)}, bf16[16,4096]{1,0:T(8,128)(2,1)S(1)}, u32[]{:S(2)}, u32[]{:S(2)}) collective-permute-start(bf16[16,4096]{1,0:T(8,128)(2,1)S(1)} %pad_maximum_fusion.2), channel_id=1, source_target_pairs={{0,4},{2,6},{4,0},{6,2},{8,12},{10,14},{12,8},{14,10},{1,5},{3,7},... | collective-permute-start | bytes 393224 | tf_op jit(solution)/shard_map/ppermute | solution.py:192
  8.6 1.5 %collective-permute-start.5 = (bf16[16,4096]{1,0:T(8,128)(2,1)S(1)}, bf16[16,4096]{1,0:T(8,128)(2,1)S(1)}, u32[]{:S(2)}, u32[]{:S(2)}) collective-permute-start(bf16[16,4096]{1,0:T(8,128)(2,1)S(1)} %pad_maximum_fusion.2), channel_id=1, source_target_pairs={{0,2},{2,0},{4,6},{6,4},{8,10},{10,8},{12,14},{14,12},{1,3},{3,1},... | collective-permute-start | bytes 393224 | tf_op jit(solution)/shard_map/ppermute | solution.py:192
  10.2 1.5 %collective-permute-start.13 = (bf16[16,4096]{1,0:T(8,128)(2,1)S(1)}, bf16[16,4096]{1,0:T(8,128)(2,1)S(1)}, u32[]{:S(2)}, u32[]{:S(2)}) collective-permute-start(bf16[16,4096]{1,0:T(8,128)(2,1)S(1)} %pad_maximum_fusion.2), channel_id=1, source_target_pairs={{0,16},{16,0},{1,17},{17,1},{2,18},{18,2},{3,19},{19,3},{4,20},{20... | collective-permute-start | bytes 393224 | tf_op jit(solution)/shard_map/ppermute | solution.py:192
  11.7 1.8 %collective-permute-done.2 = bf16[8,4096]{1,0:T(8,128)(2,1)S(1)} collective-permute-done((bf16[8,4096]{1,0:T(8,128)(2,1)S(1)}, bf16[8,4096]{1,0:T(8,128)(2,1)S(1)}, u32[]{:S(2)}, u32[]{:S(2)}) %collective-permute-start.2) | collective-permute-done | bytes 65568 | tf_op jit(solution)/shard_map/ppermute | solution.py:213
  13.5 0.8 %collective-permute-start.4 = (bf16[16,4096]{1,0:T(8,128)(2,1)S(1)}, bf16[16,4096]{1,0:T(8,128)(2,1)S(1)}, u32[]{:S(2)}, u32[]{:S(2)}) collective-permute-start(bf16[16,4096]{1,0:T(8,128)(2,1)S(1)} %pad_maximum_fusion.3), channel_id=1, source_target_pairs={{0,4},{2,6},{4,0},{6,2},{8,12},{10,14},{12,8},{14,10},{1,5},{3,7},... | collective-permute-start | bytes 393224 | tf_op jit(solution)/shard_map/ppermute | solution.py:192
  16.1 2.4 %collective-permute-done.4 = bf16[16,4096]{1,0:T(8,128)(2,1)S(1)} collective-permute-done((bf16[16,4096]{1,0:T(8,128)(2,1)S(1)}, bf16[16,4096]{1,0:T(8,128)(2,1)S(1)}, u32[]{:S(2)}, u32[]{:S(2)}) %collective-permute-start.4) | collective-permute-done | bytes 131104 | tf_op jit(solution)/shard_map/ppermute | solution.py:192
  19.1 1.6 %collective-permute-start.7 = (bf16[32,4096]{1,0:T(8,128)(2,1)S(1)}, bf16[32,4096]{1,0:T(8,128)(2,1)S(1)}, u32[]{:S(2)}, u32[]{:S(2)}) collective-permute-start(bf16[32,4096]{1,0:T(8,128)(2,1)S(1)} %constant_dynamic-update-slice_fusion), channel_id=1, source_target_pairs={{0,2},{2,0},{4,6},{6,4},{8,10},{10,8},{12,14},{14,12},{1,3},{3,1},... | collective-permute-start | bytes 786440 | tf_op jit(solution)/shard_map/ppermute | solution.py:192
  21.5 1.6 %collective-permute-start.14 = (bf16[32,4096]{1,0:T(8,128)(2,1)S(1)}, bf16[32,4096]{1,0:T(8,128)(2,1)S(1)}, u32[]{:S(2)}, u32[]{:S(2)}) collective-permute-start(bf16[32,4096]{1,0:T(8,128)(2,1)S(1)} %constant_dynamic-update-slice_fusion), channel_id=1, source_target_pairs={{0,16},{16,0},{1,17},{17,1},{2,18},{18,2},{3,19},{19,3},{4,20},{20... | collective-permute-start | bytes 786440 | tf_op jit(solution)/shard_map/ppermute | solution.py:192
  24.0 1.3 %collective-permute-start.6 = (bf16[32,2048]{1,0:T(8,128)(2,1)S(1)}, bf16[32,2048]{1,0:T(8,128)(2,1)S(1)}, u32[]{:S(2)}, u32[]{:S(2)}) collective-permute-start(bf16[32,2048]{1,0:T(8,128)(2,1)S(1)} %pad_maximum_fusion.4), channel_id=1, source_target_pairs={{0,4},{2,6},{4,0},{6,2},{8,12},{10,14},{12,8},{14,10},{1,5},{3,7},... | collective-permute-start | bytes 393224 | tf_op jit(solution)/shard_map/ppermute | solution.py:192
  25.3 0.6 %collective-permute-start.15 = (bf16[32,4096]{1,0:T(8,128)(2,1)S(1)}, bf16[32,4096]{1,0:T(8,128)(2,1)S(1)}, u32[]{:S(2)}, u32[]{:S(2)}) collective-permute-start(bf16[32,4096]{1,0:T(8,128)(2,1)S(1)} %pad_maximum_fusion.1), channel_id=1, source_target_pairs={{0,16},{16,0},{1,17},{17,1},{2,18},{18,2},{3,19},{19,3},{4,20},{20... | collective-permute-start | bytes 786440 | tf_op jit(solution)/shard_map/ppermute | solution.py:192
  25.9 1.2 %collective-permute-start.8 = (bf16[16,4096]{1,0:T(8,128)(2,1)S(1)}, bf16[16,4096]{1,0:T(8,128)(2,1)S(1)}, u32[]{:S(2)}, u32[]{:S(2)}) collective-permute-start(bf16[16,4096]{1,0:T(8,128)(2,1)S(1)} %collective-permute-done.4), channel_id=1, source_target_pairs={{0,2},{2,0},{4,6},{6,4},{8,10},{10,8},{12,14},{14,12},{1,3},{3,1},... | collective-permute-start | bytes 393224 | tf_op jit(solution)/shard_map/ppermute | solution.py:192
  27.1 3.8 %collective-permute-done.8 = bf16[16,4096]{1,0:T(8,128)(2,1)S(1)} collective-permute-done((bf16[16,4096]{1,0:T(8,128)(2,1)S(1)}, bf16[16,4096]{1,0:T(8,128)(2,1)S(1)}, u32[]{:S(2)}, u32[]{:S(2)}) %collective-permute-start.8) | collective-permute-done | bytes 131104 | tf_op jit(solution)/shard_map/ppermute | solution.py:192
  31.4 2.1 %collective-permute-done.15 = bf16[32,4096]{1,0:T(8,128)(2,1)S(1)} collective-permute-done((bf16[32,4096]{1,0:T(8,128)(2,1)S(1)}, bf16[32,4096]{1,0:T(8,128)(2,1)S(1)}, u32[]{:S(2)}, u32[]{:S(2)}) %collective-permute-start.15) | collective-permute-done | bytes 262176 | tf_op jit(solution)/shard_map/ppermute | solution.py:192
  34.2 1.6 %collective-permute-start.16 = (bf16[48,4096]{1,0:T(8,128)(2,1)S(1)}, bf16[48,4096]{1,0:T(8,128)(2,1)S(1)}, u32[]{:S(2)}, u32[]{:S(2)}) collective-permute-start(bf16[48,4096]{1,0:T(8,128)(2,1)S(1)} %get-tuple-element.40), channel_id=1, source_target_pairs={{0,16},{16,0},{1,17},{17,1},{2,18},{18,2},{3,19},{19,3},{4,20},{20... | collective-permute-start | bytes 1179656 | tf_op jit(solution)/shard_map/ppermute | solution.py:192
  37.2 3.0 %collective-permute-start.9 = (bf16[32,2048]{1,0:T(8,128)(2,1)S(1)}, bf16[32,2048]{1,0:T(8,128)(2,1)S(1)}, u32[]{:S(2)}, u32[]{:S(2)}) collective-permute-start(bf16[32,2048]{1,0:T(8,128)(2,1)S(1)} %pad_maximum_fusion.5), channel_id=1, source_target_pairs={{0,6},{2,4},{4,2},{6,0},{8,14},{10,12},{12,10},{14,8},{1,7},{3,5},... | collective-permute-start | bytes 393224 | tf_op jit(solution)/shard_map/ppermute | solution.py:192
  41.0 0.7 %collective-permute-done.10 = bf16[32,2048]{1,0:T(8,128)(2,1)S(1)} collective-permute-done((bf16[32,2048]{1,0:T(8,128)(2,1)S(1)}, bf16[32,2048]{1,0:T(8,128)(2,1)S(1)}, u32[]{:S(2)}, u32[]{:S(2)}) %collective-permute-start.10) | collective-permute-done | bytes 131104 | tf_op jit(solution)/shard_map/ppermute | solution.py:192
  41.7 1.5 %collective-permute-done.9 = bf16[32,2048]{1,0:T(8,128)(2,1)S(1)} collective-permute-done((bf16[32,2048]{1,0:T(8,128)(2,1)S(1)}, bf16[32,2048]{1,0:T(8,128)(2,1)S(1)}, u32[]{:S(2)}, u32[]{:S(2)}) %collective-permute-start.9) | collective-permute-done | bytes 131104 | tf_op jit(solution)/shard_map/ppermute | solution.py:192
  43.2 4.2 %collective-permute-start.11 = (bf16[16,2048]{1,0:T(8,128)(2,1)S(1)}, bf16[16,2048]{1,0:T(8,128)(2,1)S(1)}, u32[]{:S(2)}, u32[]{:S(2)}) collective-permute-start(bf16[16,2048]{1,0:T(8,128)(2,1)S(1)} %slice.290), channel_id=1, source_target_pairs={{0,8},{2,10},{4,12},{6,14},{8,0},{10,2},{12,4},{14,6},{1,9},{3,11}... | collective-permute-start | bytes 196616 | tf_op jit(solution)/shard_map/ppermute | solution.py:192
  47.9 1.8 %collective-permute-done.11 = bf16[16,2048]{1,0:T(8,128)(2,1)S(1)} collective-permute-done((bf16[16,2048]{1,0:T(8,128)(2,1)S(1)}, bf16[16,2048]{1,0:T(8,128)(2,1)S(1)}, u32[]{:S(2)}, u32[]{:S(2)}) %collective-permute-start.11) | collective-permute-done | bytes 65568 | tf_op jit(solution)/shard_map/ppermute | solution.py:192
  50.1 0.9 %collective-permute-done.12 = bf16[8,2048]{1,0:T(8,128)(2,1)S(1)} collective-permute-done((bf16[8,2048]{1,0:T(8,128)(2,1)S(1)}, bf16[8,2048]{1,0:T(8,128)(2,1)S(1)}, u32[]{:S(2)}, u32[]{:S(2)}) %collective-permute-start.12) | collective-permute-done | bytes 32800 | tf_op jit(solution)/shard_map/ppermute | solution.py:192
  51.0 1.1 %convolution_convert_fusion = bf16[128,2048]{1,0:T(8,128)(2,1)} fusion(bf16[16,128]{1,0:T(8,128)(2,1)S(1)} %get-tuple-element.12, bf16[8,2048]{1,0:T(8,128)(2,1)S(1)} %collective-permute-done.12, bf16[8,2048]{1,0:T(8,128)(2,1)S(1)} %get-tuple-element.53), kind=kOutput, calls=%fused_computation | convolution fusion | flops 8781824 | bytes 593920 | tf_op jit(solution)/shard_map/dot_general | solution.py:260
  52.8 1.6 %finish.1 = (bf16[2048,128]{1,0:T(8,128)(2,1)}, bf16[2048,128]{1,0:T(8,128)(2,1)}, bf16[128,2048]{1,0:T(8,128)(2,1)}) custom-call(f32[2048,128]{1,0:T(8,128)S(1)} %fusion.5.gate_ref, f32[2048,128]{1,0:T(8,128)S(1)} %fusion.3.up_ref, f32[128,2048]{1,0:T(8,128)S(1)} %fusion.1.down_ref, bf16[48,4096]{1,0:T(8,128)(2,1)S(1)} %collective-permute-done.16.rows_ref, ...), custom_call_target="tpu_custom_call" | custom-call | tf_op jit(solution)/shard_map/finish/pallas_call | solution.py:171
  (89 shorter events, 9.7 us)
Async XLA Ops:
  0.6 14.2 %copy-start = (bf16[1,2048,128]{2,1,0:T(8,128)(2,1)S(1)}, bf16[1,2048,128]{2,1,0:T(8,128)(2,1)}, u32[]{:S(2)}) copy-start(bf16[1,2048,128]{2,1,0:T(8,128)(2,1)} %param.11) | copy-start | bytes 1572868
  0.6 13.7 %copy-start.2 = (bf16[1,128,2048]{2,1,0:T(8,128)(2,1)S(1)}, bf16[1,128,2048]{2,1,0:T(8,128)(2,1)}, u32[]{:S(2)}) copy-start(bf16[1,128,2048]{2,1,0:T(8,128)(2,1)} %param.13) | copy-start | bytes 1572868
  0.7 13.9 %copy-start.1 = (bf16[1,2048,128]{2,1,0:T(8,128)(2,1)S(1)}, bf16[1,2048,128]{2,1,0:T(8,128)(2,1)}, u32[]{:S(2)}) copy-start(bf16[1,2048,128]{2,1,0:T(8,128)(2,1)} %param.12) | copy-start | bytes 1572868
  2.4 4.3 %collective-permute-start = (bf16[8,4096]{1,0:T(8,128)(2,1)S(1)}, bf16[8,4096]{1,0:T(8,128)(2,1)S(1)}, u32[]{:S(2)}, u32[]{:S(2)}) collective-permute-start(bf16[8,4096]{1,0:T(8,128)(2,1)S(1)} %get-tuple-element.46), channel_id=1, source_target_pairs={{0,1},{1,0},{2,3},{3,2},{4,5},{5,4},{6,7},{7,6},{8,9},{9,8},{10,11... | collective-permute-start | bytes 196616 | tf_op jit(solution)/shard_map/ppermute | solution.py:192
  3.0 10.5 %collective-permute-start.3 = (bf16[8,4096]{1,0:T(8,128)(2,1)S(1)}, bf16[8,4096]{1,0:T(8,128)(2,1)S(1)}, u32[]{:S(2)}, u32[]{:S(2)}) collective-permute-start(bf16[8,4096]{1,0:T(8,128)(2,1)S(1)} %get-tuple-element.46), channel_id=1, source_target_pairs={{0,9},{1,8},{2,11},{3,10},{4,13},{5,12},{6,15},{7,14},{8,1},{9,0},... | collective-permute-start | bytes 196616 | tf_op jit(solution)/shard_map/ppermute | solution.py:213
  6.7 6.8 %collective-permute-start.2 = (bf16[8,4096]{1,0:T(8,128)(2,1)S(1)}, bf16[8,4096]{1,0:T(8,128)(2,1)S(1)}, u32[]{:S(2)}, u32[]{:S(2)}) collective-permute-start(bf16[8,4096]{1,0:T(8,128)(2,1)S(1)} %get-tuple-element.47), channel_id=1, source_target_pairs={{0,8},{1,9},{2,10},{3,11},{4,12},{5,13},{6,14},{7,15},{8,0},{9,1},... | collective-permute-start | bytes 196616 | tf_op jit(solution)/shard_map/ppermute | solution.py:213
  6.7 8.8 %collective-permute-start.1 = (bf16[16,4096]{1,0:T(8,128)(2,1)S(1)}, bf16[16,4096]{1,0:T(8,128)(2,1)S(1)}, u32[]{:S(2)}, u32[]{:S(2)}) collective-permute-start(bf16[16,4096]{1,0:T(8,128)(2,1)S(1)} %pad_maximum_fusion.2), channel_id=1, source_target_pairs={{0,4},{2,6},{4,0},{6,2},{8,12},{10,14},{12,8},{14,10},{1,5},{3,7},... | collective-permute-start | bytes 393224 | tf_op jit(solution)/shard_map/ppermute | solution.py:192
  8.6 7.2 %collective-permute-start.5 = (bf16[16,4096]{1,0:T(8,128)(2,1)S(1)}, bf16[16,4096]{1,0:T(8,128)(2,1)S(1)}, u32[]{:S(2)}, u32[]{:S(2)}) collective-permute-start(bf16[16,4096]{1,0:T(8,128)(2,1)S(1)} %pad_maximum_fusion.2), channel_id=1, source_target_pairs={{0,2},{2,0},{4,6},{6,4},{8,10},{10,8},{12,14},{14,12},{1,3},{3,1},... | collective-permute-start | bytes 393224 | tf_op jit(solution)/shard_map/ppermute | solution.py:192
  10.2 21.2 %collective-permute-start.13 = (bf16[16,4096]{1,0:T(8,128)(2,1)S(1)}, bf16[16,4096]{1,0:T(8,128)(2,1)S(1)}, u32[]{:S(2)}, u32[]{:S(2)}) collective-permute-start(bf16[16,4096]{1,0:T(8,128)(2,1)S(1)} %pad_maximum_fusion.2), channel_id=1, source_target_pairs={{0,16},{16,0},{1,17},{17,1},{2,18},{18,2},{3,19},{19,3},{4,20},{20... | collective-permute-start | bytes 393224 | tf_op jit(solution)/shard_map/ppermute | solution.py:192
  13.5 5.0 %collective-permute-start.4 = (bf16[16,4096]{1,0:T(8,128)(2,1)S(1)}, bf16[16,4096]{1,0:T(8,128)(2,1)S(1)}, u32[]{:S(2)}, u32[]{:S(2)}) collective-permute-start(bf16[16,4096]{1,0:T(8,128)(2,1)S(1)} %pad_maximum_fusion.3), channel_id=1, source_target_pairs={{0,4},{2,6},{4,0},{6,2},{8,12},{10,14},{12,8},{14,10},{1,5},{3,7},... | collective-permute-start | bytes 393224 | tf_op jit(solution)/shard_map/ppermute | solution.py:192
  19.1 6.8 %collective-permute-start.7 = (bf16[32,4096]{1,0:T(8,128)(2,1)S(1)}, bf16[32,4096]{1,0:T(8,128)(2,1)S(1)}, u32[]{:S(2)}, u32[]{:S(2)}) collective-permute-start(bf16[32,4096]{1,0:T(8,128)(2,1)S(1)} %constant_dynamic-update-slice_fusion), channel_id=1, source_target_pairs={{0,2},{2,0},{4,6},{6,4},{8,10},{10,8},{12,14},{14,12},{1,3},{3,1},... | collective-permute-start | bytes 786440 | tf_op jit(solution)/shard_map/ppermute | solution.py:192
  21.5 9.9 %collective-permute-start.14 = (bf16[32,4096]{1,0:T(8,128)(2,1)S(1)}, bf16[32,4096]{1,0:T(8,128)(2,1)S(1)}, u32[]{:S(2)}, u32[]{:S(2)}) collective-permute-start(bf16[32,4096]{1,0:T(8,128)(2,1)S(1)} %constant_dynamic-update-slice_fusion), channel_id=1, source_target_pairs={{0,16},{16,0},{1,17},{17,1},{2,18},{18,2},{3,19},{19,3},{4,20},{20... | collective-permute-start | bytes 786440 | tf_op jit(solution)/shard_map/ppermute | solution.py:192
  24.0 17.0 %collective-permute-start.6 = (bf16[32,2048]{1,0:T(8,128)(2,1)S(1)}, bf16[32,2048]{1,0:T(8,128)(2,1)S(1)}, u32[]{:S(2)}, u32[]{:S(2)}) collective-permute-start(bf16[32,2048]{1,0:T(8,128)(2,1)S(1)} %pad_maximum_fusion.4), channel_id=1, source_target_pairs={{0,4},{2,6},{4,0},{6,2},{8,12},{10,14},{12,8},{14,10},{1,5},{3,7},... | collective-permute-start | bytes 393224 | tf_op jit(solution)/shard_map/ppermute | solution.py:192
  25.3 8.3 %collective-permute-start.15 = (bf16[32,4096]{1,0:T(8,128)(2,1)S(1)}, bf16[32,4096]{1,0:T(8,128)(2,1)S(1)}, u32[]{:S(2)}, u32[]{:S(2)}) collective-permute-start(bf16[32,4096]{1,0:T(8,128)(2,1)S(1)} %pad_maximum_fusion.1), channel_id=1, source_target_pairs={{0,16},{16,0},{1,17},{17,1},{2,18},{18,2},{3,19},{19,3},{4,20},{20... | collective-permute-start | bytes 786440 | tf_op jit(solution)/shard_map/ppermute | solution.py:192
  25.9 5.0 %collective-permute-start.8 = (bf16[16,4096]{1,0:T(8,128)(2,1)S(1)}, bf16[16,4096]{1,0:T(8,128)(2,1)S(1)}, u32[]{:S(2)}, u32[]{:S(2)}) collective-permute-start(bf16[16,4096]{1,0:T(8,128)(2,1)S(1)} %collective-permute-done.4), channel_id=1, source_target_pairs={{0,2},{2,0},{4,6},{6,4},{8,10},{10,8},{12,14},{14,12},{1,3},{3,1},... | collective-permute-start | bytes 393224 | tf_op jit(solution)/shard_map/ppermute | solution.py:192
  34.2 17.9 %collective-permute-start.16 = (bf16[48,4096]{1,0:T(8,128)(2,1)S(1)}, bf16[48,4096]{1,0:T(8,128)(2,1)S(1)}, u32[]{:S(2)}, u32[]{:S(2)}) collective-permute-start(bf16[48,4096]{1,0:T(8,128)(2,1)S(1)} %get-tuple-element.40), channel_id=1, source_target_pairs={{0,16},{16,0},{1,17},{17,1},{2,18},{18,2},{3,19},{19,3},{4,20},{20... | collective-permute-start | bytes 1179656 | tf_op jit(solution)/shard_map/ppermute | solution.py:192
  36.6 5.0 %collective-permute-start.10 = (bf16[32,2048]{1,0:T(8,128)(2,1)S(1)}, bf16[32,2048]{1,0:T(8,128)(2,1)S(1)}, u32[]{:S(2)}, u32[]{:S(2)}) collective-permute-start(bf16[32,2048]{1,0:T(8,128)(2,1)S(1)} %pad_maximum_fusion.6), channel_id=1, source_target_pairs={{0,2},{2,0},{4,6},{6,4},{8,10},{10,8},{12,14},{14,12},{1,3},{3,1},... | collective-permute-start | bytes 393224 | tf_op jit(solution)/shard_map/ppermute | solution.py:192
  37.2 5.9 %collective-permute-start.9 = (bf16[32,2048]{1,0:T(8,128)(2,1)S(1)}, bf16[32,2048]{1,0:T(8,128)(2,1)S(1)}, u32[]{:S(2)}, u32[]{:S(2)}) collective-permute-start(bf16[32,2048]{1,0:T(8,128)(2,1)S(1)} %pad_maximum_fusion.5), channel_id=1, source_target_pairs={{0,6},{2,4},{4,2},{6,0},{8,14},{10,12},{12,10},{14,8},{1,7},{3,5},... | collective-permute-start | bytes 393224 | tf_op jit(solution)/shard_map/ppermute | solution.py:192
  43.2 6.4 %collective-permute-start.11 = (bf16[16,2048]{1,0:T(8,128)(2,1)S(1)}, bf16[16,2048]{1,0:T(8,128)(2,1)S(1)}, u32[]{:S(2)}, u32[]{:S(2)}) collective-permute-start(bf16[16,2048]{1,0:T(8,128)(2,1)S(1)} %slice.290), channel_id=1, source_target_pairs={{0,8},{2,10},{4,12},{6,14},{8,0},{10,2},{12,4},{14,6},{1,9},{3,11}... | collective-permute-start | bytes 196616 | tf_op jit(solution)/shard_map/ppermute | solution.py:192
  49.7 1.3 %collective-permute-start.12 = (bf16[8,2048]{1,0:T(8,128)(2,1)S(1)}, bf16[8,2048]{1,0:T(8,128)(2,1)S(1)}, u32[]{:S(2)}, u32[]{:S(2)}) collective-permute-start(bf16[8,2048]{1,0:T(8,128)(2,1)S(1)} %get-tuple-element.54), channel_id=1, source_target_pairs={{0,1},{1,0},{2,3},{3,2},{4,5},{5,4},{6,7},{7,6},{8,9},{9,8},{10,11... | collective-permute-start | bytes 98312 | tf_op jit(solution)/shard_map/ppermute | solution.py:192

commit v3 on v2

--- a/solution.py
+++ b/solution.py
@@ -14,7 +14,7 @@
 
 
 FRONT_VMEM = 55000 << 10
-CHUNKS = 4
+CHUNKS = 1
 
 NT = (((1,), (1,)), ((), ()))
 TN = (((0,), (0,)), ((), ()))
@@ -200,17 +200,19 @@
         pltpu.with_memory_space_constraint(gate_probs.T, pltpu.HBM),
         tokens, cotangent, window
     )
-    split = [rows[index * CAP : (index + 1) * CAP] for index in range(window)]
-    near = [split[0]]
-    for index in range(1, window):
-        near.append(swap(split[index], "win", index))
-    far = []
-    for index in range(window):
+
+    def send_far(value, index):
         pairs = []
         for s in range(SLICES):
             for e in range(window):
                 pairs.append((s * window + e, (s ^ FAR) * window + (e ^ index)))
-        far.append(lax.ppermute(split[index], ("slice", "win"), pairs))
+        return lax.ppermute(value, ("slice", "win"), pairs)
+
+    parcels = [rows[index * CAP : (index + 1) * CAP] for index in range(window)]
+    near = [parcels[0]]
+    for index in range(1, window):
+        near.append(swap(parcels[index], "win", index))
+    far = [send_far(item, index) for index, item in enumerate(parcels)]
 
     rows = {0: join(near), FAR: join(far)}
 
@@ -247,16 +249,24 @@
     back = lax.optimization_barrier(join([parts[0], parts[4]]))
     turn(6, 1)
     turn(3, 5, 7)
-    incoming = [give(mask) for mask in (2, 3, 1)]
+    incoming = [give(mask) for mask in (2, 3)]
+    halves = [swap(parts[mask].astype(jnp.bfloat16), "slice", 1) for mask in (1, 1 ^ FAR)]
+    incoming.append(join(halves))
     last = parts[7]
     for part in incoming:
         back = back + part.astype(jnp.float32)
 
-    far = swap(back[block:].astype(jnp.bfloat16), "slice", FAR)
-    back = (back[:block] + far.astype(jnp.float32)).astype(jnp.bfloat16)
-    kept = [back[:CAP]]
-    for index in range(1, window):
-        kept.append(swap(back[index * CAP : (index + 1) * CAP], "win", index))
+    def split(value):
+        return [value[index * CAP : (index + 1) * CAP] for index in range(window)]
+
+    here, there = split(back[:block]), split(back[block:].astype(jnp.bfloat16))
+    kept = []
+    for index in range(window):
+        theirs = send_far(there[index], index)
+        mine = here[index]
+        if index:
+            mine = swap(mine.astype(jnp.bfloat16), "win", index)
+        kept.append((mine.astype(jnp.float32) + theirs.astype(jnp.float32)).astype(jnp.bfloat16))
     grad_input = lax.dot_general(
         picker, join(kept), TN, preferred_element_type=jnp.float32
     ).astype(jnp.bfloat16)

time: 54.6 us -> 61.4 us (1.12)
  waiting for transfers between devices: 15 us -> 19.9 us
  starting transfers between devices: 25.5 us -> 27.6 us
    ppermute x2 -> x4, waiting for transfers between devices: 1.84 us -> 5.93 us  [send_far(): return lax.ppermute(value, ('slice', 'win'), pairs)]
    ppermute x2 -> x4, starting transfers between devices: 3.73 us -> 7.05 us  [send_far(): return lax.ppermute(value, ('slice', 'win'), pairs)]
    ppermute x15, starting transfers between devices: 21.8 us -> 20.6 us  [swap(): return lax.ppermute(value, axis, pairs)]
    ppermute x15, waiting for transfers between devices: 13.2 us -> 13.9 us  [swap(): return lax.ppermute(value, axis, pairs)]
  transfers between devices with their start and end apart: 17 -> 19, of which waited for: 8 -> 9; matrix products, arithmetic and copies ran while one was open for 16% -> 14% of each run, Pallas kernels for 0% -> 0%
where the time goes in v3:
time: 61.4 us; the launch traced here: 61.3 us
  starting transfers between devices  27.6 us (45%)
  waiting for transfers between devices  19.9 us (32%)
  matrix products  8.9 us (14%)
  Pallas kernels  3.19 us (5%)
  between operations  1.04 us (2%)
    ppermute x15, starting transfers between devices, swap(): return lax.ppermute(value, axis, pairs)  20.6 us
    ppermute x15, waiting for transfers between devices, swap(): return lax.ppermute(value, axis, pairs)  13.9 us
    ppermute x4, starting transfers between devices, send_far(): return lax.ppermute(value, ('slice', 'win'), pairs)  7.05 us
    ppermute x4, waiting for transfers between devices, send_far(): return lax.ppermute(value, ('slice', 'win'), pairs)  5.93 us
    dot_general x6, matrix products, hidden(): lax.dot_general(rows_cot, down_rows, NT, preferred_element_type=jnp.float32)  1.72 us
    pallas_call x1, Pallas kernels, finish(): pl.pallas_call(finish_kernel, out_shape=tuple((jax.ShapeDtypeStruct(g.sha...  1.6 us
    pallas_call x1, Pallas kernels, front(): pl.pallas_call(functools.partial(front_kernel, window), out_shape=(jax.Sh...  1.6 us
    dot_general x6, matrix products, hidden(): gate_pre = jnp.dot(rows_in, gate_rows, preferred_element_type=jnp.float32)  1.32 us
  transfers between devices with their start and end apart: 19, of which 9 were waited for; matrix products, arithmetic and copies ran while one was open for 14% of the time, Pallas kernels for 0%

profile of v3, /device:TPU:0, one launch (start us, length us, event | category | flops | bytes accessed | tf_op | source)
XLA Modules:
  0.0 61.3 jit_solution(6788078001054723056)
XLA Ops:
  0.7 1.6 %front.1 = (bf16[16,4096]{1,0:T(8,128)(2,1)S(1)}, bf16[16,128]{1,0:T(8,128)(2,1)S(1)}) custom-call(s32[1]{0:T(128)} %bitcast.mine_ref, s32[8,128]{1,0:T(8,128)} %bitcast.85, f32[8,128]{1,0:T(8,128)} %bitcast.86, bf16[128,2048]{1,0:T(8,128)(2,1)} %tokens_hbm.1, bf16[128,2048]{1,0:T(8,128)(2,1)} %cot_hbm.1), custom_call_target="tpu_custom_call" | custom-call | tf_op jit(solution)/shard_map/front/pallas_call | solution.py:114
  2.9 3.7 %collective-permute-start.3 = (bf16[8,4096]{1,0:T(8,128)(2,1)S(1)}, bf16[8,4096]{1,0:T(8,128)(2,1)S(1)}, u32[]{:S(2)}, u32[]{:S(2)}) collective-permute-start(bf16[8,4096]{1,0:T(8,128)(2,1)S(1)} %get-tuple-element.48), channel_id=1, source_target_pairs={{0,9},{1,8},{2,11},{3,10},{4,13},{5,12},{6,15},{7,14},{8,1},{9,0},... | collective-permute-start | bytes 196616 | tf_op jit(solution)/shard_map/ppermute | solution.py:209
  6.6 1.9 %collective-permute-start.1 = (bf16[16,4096]{1,0:T(8,128)(2,1)S(1)}, bf16[16,4096]{1,0:T(8,128)(2,1)S(1)}, u32[]{:S(2)}, u32[]{:S(2)}) collective-permute-start(bf16[16,4096]{1,0:T(8,128)(2,1)S(1)} %pad_maximum_fusion.2), channel_id=1, source_target_pairs={{0,4},{2,6},{4,0},{6,2},{8,12},{10,14},{12,8},{14,10},{1,5},{3,7},... | collective-permute-start | bytes 393224 | tf_op jit(solution)/shard_map/ppermute | solution.py:192
  8.5 1.5 %collective-permute-start.5 = (bf16[16,4096]{1,0:T(8,128)(2,1)S(1)}, bf16[16,4096]{1,0:T(8,128)(2,1)S(1)}, u32[]{:S(2)}, u32[]{:S(2)}) collective-permute-start(bf16[16,4096]{1,0:T(8,128)(2,1)S(1)} %pad_maximum_fusion.2), channel_id=1, source_target_pairs={{0,2},{2,0},{4,6},{6,4},{8,10},{10,8},{12,14},{14,12},{1,3},{3,1},... | collective-permute-start | bytes 393224 | tf_op jit(solution)/shard_map/ppermute | solution.py:192
  10.1 1.5 %collective-permute-start.15 = (bf16[16,4096]{1,0:T(8,128)(2,1)S(1)}, bf16[16,4096]{1,0:T(8,128)(2,1)S(1)}, u32[]{:S(2)}, u32[]{:S(2)}) collective-permute-start(bf16[16,4096]{1,0:T(8,128)(2,1)S(1)} %pad_maximum_fusion.2), channel_id=1, source_target_pairs={{0,16},{16,0},{1,17},{17,1},{2,18},{18,2},{3,19},{19,3},{4,20},{20... | collective-permute-start | bytes 393224 | tf_op jit(solution)/shard_map/ppermute | solution.py:192
  11.6 1.8 %collective-permute-done.2 = bf16[8,4096]{1,0:T(8,128)(2,1)S(1)} collective-permute-done((bf16[8,4096]{1,0:T(8,128)(2,1)S(1)}, bf16[8,4096]{1,0:T(8,128)(2,1)S(1)}, u32[]{:S(2)}, u32[]{:S(2)}) %collective-permute-start.2) | collective-permute-done | bytes 65568 | tf_op jit(solution)/shard_map/ppermute | solution.py:209
  13.4 0.8 %collective-permute-start.4 = (bf16[16,4096]{1,0:T(8,128)(2,1)S(1)}, bf16[16,4096]{1,0:T(8,128)(2,1)S(1)}, u32[]{:S(2)}, u32[]{:S(2)}) collective-permute-start(bf16[16,4096]{1,0:T(8,128)(2,1)S(1)} %pad_maximum_fusion.3), channel_id=1, source_target_pairs={{0,4},{2,6},{4,0},{6,2},{8,12},{10,14},{12,8},{14,10},{1,5},{3,7},... | collective-permute-start | bytes 393224 | tf_op jit(solution)/shard_map/ppermute | solution.py:192
  16.0 2.4 %collective-permute-done.4 = bf16[16,4096]{1,0:T(8,128)(2,1)S(1)} collective-permute-done((bf16[16,4096]{1,0:T(8,128)(2,1)S(1)}, bf16[16,4096]{1,0:T(8,128)(2,1)S(1)}, u32[]{:S(2)}, u32[]{:S(2)}) %collective-permute-start.4) | collective-permute-done | bytes 131104 | tf_op jit(solution)/shard_map/ppermute | solution.py:192
  19.0 1.6 %collective-permute-start.7 = (bf16[32,4096]{1,0:T(8,128)(2,1)S(1)}, bf16[32,4096]{1,0:T(8,128)(2,1)S(1)}, u32[]{:S(2)}, u32[]{:S(2)}) collective-permute-start(bf16[32,4096]{1,0:T(8,128)(2,1)S(1)} %constant_dynamic-update-slice_fusion), channel_id=1, source_target_pairs={{0,2},{2,0},{4,6},{6,4},{8,10},{10,8},{12,14},{14,12},{1,3},{3,1},... | collective-permute-start | bytes 786440 | tf_op jit(solution)/shard_map/ppermute | solution.py:192
  21.4 1.6 %collective-permute-start.16 = (bf16[32,4096]{1,0:T(8,128)(2,1)S(1)}, bf16[32,4096]{1,0:T(8,128)(2,1)S(1)}, u32[]{:S(2)}, u32[]{:S(2)}) collective-permute-start(bf16[32,4096]{1,0:T(8,128)(2,1)S(1)} %constant_dynamic-update-slice_fusion), channel_id=1, source_target_pairs={{0,16},{16,0},{1,17},{17,1},{2,18},{18,2},{3,19},{19,3},{4,20},{20... | collective-permute-start | bytes 786440 | tf_op jit(solution)/shard_map/ppermute | solution.py:192
  24.4 1.3 %collective-permute-start.6 = (bf16[32,2048]{1,0:T(8,128)(2,1)S(1)}, bf16[32,2048]{1,0:T(8,128)(2,1)S(1)}, u32[]{:S(2)}, u32[]{:S(2)}) collective-permute-start(bf16[32,2048]{1,0:T(8,128)(2,1)S(1)} %pad_maximum_fusion.4), channel_id=1, source_target_pairs={{0,4},{2,6},{4,0},{6,2},{8,12},{10,14},{12,8},{14,10},{1,5},{3,7},... | collective-permute-start | bytes 393224 | tf_op jit(solution)/shard_map/ppermute | solution.py:192
  26.1 1.6 %collective-permute-start.8 = (bf16[16,4096]{1,0:T(8,128)(2,1)S(1)}, bf16[16,4096]{1,0:T(8,128)(2,1)S(1)}, u32[]{:S(2)}, u32[]{:S(2)}) collective-permute-start(bf16[16,4096]{1,0:T(8,128)(2,1)S(1)} %collective-permute-done.4), channel_id=1, source_target_pairs={{0,2},{2,0},{4,6},{6,4},{8,10},{10,8},{12,14},{14,12},{1,3},{3,1},... | collective-permute-start | bytes 393224 | tf_op jit(solution)/shard_map/ppermute | solution.py:192
  27.7 3.4 %collective-permute-done.8 = bf16[16,4096]{1,0:T(8,128)(2,1)S(1)} collective-permute-done((bf16[16,4096]{1,0:T(8,128)(2,1)S(1)}, bf16[16,4096]{1,0:T(8,128)(2,1)S(1)}, u32[]{:S(2)}, u32[]{:S(2)}) %collective-permute-start.8) | collective-permute-done | bytes 131104 | tf_op jit(solution)/shard_map/ppermute | solution.py:192
  31.0 2.1 %collective-permute-start.17 = (bf16[32,4096]{1,0:T(8,128)(2,1)S(1)}, bf16[32,4096]{1,0:T(8,128)(2,1)S(1)}, u32[]{:S(2)}, u32[]{:S(2)}) collective-permute-start(bf16[32,4096]{1,0:T(8,128)(2,1)S(1)} %pad_maximum_fusion.1), channel_id=1, source_target_pairs={{0,16},{16,0},{1,17},{17,1},{2,18},{18,2},{3,19},{19,3},{4,20},{20... | collective-permute-start | bytes 786440 | tf_op jit(solution)/shard_map/ppermute | solution.py:192
  33.7 4.5 %collective-permute-done.17 = bf16[32,4096]{1,0:T(8,128)(2,1)S(1)} collective-permute-done((bf16[32,4096]{1,0:T(8,128)(2,1)S(1)}, bf16[32,4096]{1,0:T(8,128)(2,1)S(1)}, u32[]{:S(2)}, u32[]{:S(2)}) %collective-permute-start.17) | collective-permute-done | bytes 262176 | tf_op jit(solution)/shard_map/ppermute | solution.py:192
  38.9 2.5 %collective-permute-start.18 = (bf16[48,4096]{1,0:T(8,128)(2,1)S(1)}, bf16[48,4096]{1,0:T(8,128)(2,1)S(1)}, u32[]{:S(2)}, u32[]{:S(2)}) collective-permute-start(bf16[48,4096]{1,0:T(8,128)(2,1)S(1)} %get-tuple-element.42), channel_id=1, source_target_pairs={{0,16},{16,0},{1,17},{17,1},{2,18},{18,2},{3,19},{19,3},{4,20},{20... | collective-permute-start | bytes 1179656 | tf_op jit(solution)/shard_map/ppermute | solution.py:192
  42.3 1.6 %collective-permute-start.11 = (bf16[16,2048]{1,0:T(8,128)(2,1)S(1)}, bf16[16,2048]{1,0:T(8,128)(2,1)S(1)}, u32[]{:S(2)}, u32[]{:S(2)}) collective-permute-start(bf16[16,2048]{1,0:T(8,128)(2,1)S(1)} %get-tuple-element.38), channel_id=1, source_target_pairs={{0,2},{2,0},{4,6},{6,4},{8,10},{10,8},{12,14},{14,12},{1,3},{3,1},... | collective-permute-start | bytes 196616 | tf_op jit(solution)/shard_map/ppermute | solution.py:192
  43.9 1.3 %collective-permute-start.9 = (bf16[32,2048]{1,0:T(8,128)(2,1)S(1)}, bf16[32,2048]{1,0:T(8,128)(2,1)S(1)}, u32[]{:S(2)}, u32[]{:S(2)}) collective-permute-start(bf16[32,2048]{1,0:T(8,128)(2,1)S(1)} %pad_maximum_fusion.5), channel_id=1, source_target_pairs={{0,6},{2,4},{4,2},{6,0},{8,14},{10,12},{12,10},{14,8},{1,7},{3,5},... | collective-permute-start | bytes 393224 | tf_op jit(solution)/shard_map/ppermute | solution.py:192
  46.6 3.2 %collective-permute-done.9 = bf16[32,2048]{1,0:T(8,128)(2,1)S(1)} collective-permute-done((bf16[32,2048]{1,0:T(8,128)(2,1)S(1)}, bf16[32,2048]{1,0:T(8,128)(2,1)S(1)}, u32[]{:S(2)}, u32[]{:S(2)}) %collective-permute-start.9) | collective-permute-done | bytes 131104 | tf_op jit(solution)/shard_map/ppermute | solution.py:192
  49.9 3.3 %collective-permute-start.12 = (bf16[8,2048]{1,0:T(8,128)(2,1)S(1)}, bf16[8,2048]{1,0:T(8,128)(2,1)S(1)}, u32[]{:S(2)}, u32[]{:S(2)}) collective-permute-start(bf16[8,2048]{1,0:T(8,128)(2,1)S(1)} %get-tuple-element.50), channel_id=1, source_target_pairs={{0,8},{1,9},{2,10},{3,11},{4,12},{5,13},{6,14},{7,15},{8,0},{9,1},... | collective-permute-start | bytes 98312 | tf_op jit(solution)/shard_map/ppermute | solution.py:209
  53.7 1.4 %collective-permute-done.12 = bf16[8,2048]{1,0:T(8,128)(2,1)S(1)} collective-permute-done((bf16[8,2048]{1,0:T(8,128)(2,1)S(1)}, bf16[8,2048]{1,0:T(8,128)(2,1)S(1)}, u32[]{:S(2)}, u32[]{:S(2)}) %collective-permute-start.12) | collective-permute-done | bytes 32800 | tf_op jit(solution)/shard_map/ppermute | solution.py:209
  55.1 2.7 %collective-permute-done.14 = bf16[8,2048]{1,0:T(8,128)(2,1)S(1)} collective-permute-done((bf16[8,2048]{1,0:T(8,128)(2,1)S(1)}, bf16[8,2048]{1,0:T(8,128)(2,1)S(1)}, u32[]{:S(2)}, u32[]{:S(2)}) %collective-permute-start.14) | collective-permute-done | bytes 32800 | tf_op jit(solution)/shard_map/ppermute | solution.py:209
  57.8 1.1 %convolution_convert_fusion = bf16[128,2048]{1,0:T(8,128)(2,1)} fusion(bf16[16,128]{1,0:T(8,128)(2,1)S(1)} %get-tuple-element.12, bf16[8,2048]{1,0:T(8,128)(2,1)S(1)} %add_convert_fusion, bf16[8,2048]{1,0:T(8,128)(2,1)S(1)} %fusion.73), kind=kOutput, calls=%fused_computation | convolution fusion | flops 8781824 | bytes 593920 | tf_op jit(solution)/shard_map/dot_general | solution.py:270
  59.7 1.6 %finish.1 = (bf16[2048,128]{1,0:T(8,128)(2,1)}, bf16[2048,128]{1,0:T(8,128)(2,1)}, bf16[128,2048]{1,0:T(8,128)(2,1)}) custom-call(f32[2048,128]{1,0:T(8,128)S(1)} %fusion.5.gate_ref, f32[2048,128]{1,0:T(8,128)S(1)} %fusion.3.up_ref, f32[128,2048]{1,0:T(8,128)S(1)} %fusion.1.down_ref, bf16[48,4096]{1,0:T(8,128)(2,1)S(1)} %collective-permute-done.18.rows_ref, ...), custom_call_target="tpu_custom_call" | custom-call | tf_op jit(solution)/shard_map/finish/pallas_call | solution.py:171
  (92 shorter events, 10.3 us)
Async XLA Ops:
  0.6 14.1 %copy-start = (bf16[1,2048,128]{2,1,0:T(8,128)(2,1)S(1)}, bf16[1,2048,128]{2,1,0:T(8,128)(2,1)}, u32[]{:S(2)}) copy-start(bf16[1,2048,128]{2,1,0:T(8,128)(2,1)} %param.11) | copy-start | bytes 1572868
  0.6 13.6 %copy-start.2 = (bf16[1,128,2048]{2,1,0:T(8,128)(2,1)S(1)}, bf16[1,128,2048]{2,1,0:T(8,128)(2,1)}, u32[]{:S(2)}) copy-start(bf16[1,128,2048]{2,1,0:T(8,128)(2,1)} %param.13) | copy-start | bytes 1572868
  0.7 13.8 %copy-start.1 = (bf16[1,2048,128]{2,1,0:T(8,128)(2,1)S(1)}, bf16[1,2048,128]{2,1,0:T(8,128)(2,1)}, u32[]{:S(2)}) copy-start(bf16[1,2048,128]{2,1,0:T(8,128)(2,1)} %param.12) | copy-start | bytes 1572868
  2.3 4.3 %collective-permute-start = (bf16[8,4096]{1,0:T(8,128)(2,1)S(1)}, bf16[8,4096]{1,0:T(8,128)(2,1)S(1)}, u32[]{:S(2)}, u32[]{:S(2)}) collective-permute-start(bf16[8,4096]{1,0:T(8,128)(2,1)S(1)} %get-tuple-element.48), channel_id=1, source_target_pairs={{0,1},{1,0},{2,3},{3,2},{4,5},{5,4},{6,7},{7,6},{8,9},{9,8},{10,11... | collective-permute-start | bytes 196616 | tf_op jit(solution)/shard_map/ppermute | solution.py:192
  2.9 10.5 %collective-permute-start.3 = (bf16[8,4096]{1,0:T(8,128)(2,1)S(1)}, bf16[8,4096]{1,0:T(8,128)(2,1)S(1)}, u32[]{:S(2)}, u32[]{:S(2)}) collective-permute-start(bf16[8,4096]{1,0:T(8,128)(2,1)S(1)} %get-tuple-element.48), channel_id=1, source_target_pairs={{0,9},{1,8},{2,11},{3,10},{4,13},{5,12},{6,15},{7,14},{8,1},{9,0},... | collective-permute-start | bytes 196616 | tf_op jit(solution)/shard_map/ppermute | solution.py:209
  6.5 6.8 %collective-permute-start.2 = (bf16[8,4096]{1,0:T(8,128)(2,1)S(1)}, bf16[8,4096]{1,0:T(8,128)(2,1)S(1)}, u32[]{:S(2)}, u32[]{:S(2)}) collective-permute-start(bf16[8,4096]{1,0:T(8,128)(2,1)S(1)} %get-tuple-element.49), channel_id=1, source_target_pairs={{0,8},{1,9},{2,10},{3,11},{4,12},{5,13},{6,14},{7,15},{8,0},{9,1},... | collective-permute-start | bytes 196616 | tf_op jit(solution)/shard_map/ppermute | solution.py:209
  6.6 8.8 %collective-permute-start.1 = (bf16[16,4096]{1,0:T(8,128)(2,1)S(1)}, bf16[16,4096]{1,0:T(8,128)(2,1)S(1)}, u32[]{:S(2)}, u32[]{:S(2)}) collective-permute-start(bf16[16,4096]{1,0:T(8,128)(2,1)S(1)} %pad_maximum_fusion.2), channel_id=1, source_target_pairs={{0,4},{2,6},{4,0},{6,2},{8,12},{10,14},{12,8},{14,10},{1,5},{3,7},... | collective-permute-start | bytes 393224 | tf_op jit(solution)/shard_map/ppermute | solution.py:192
  8.5 7.2 %collective-permute-start.5 = (bf16[16,4096]{1,0:T(8,128)(2,1)S(1)}, bf16[16,4096]{1,0:T(8,128)(2,1)S(1)}, u32[]{:S(2)}, u32[]{:S(2)}) collective-permute-start(bf16[16,4096]{1,0:T(8,128)(2,1)S(1)} %pad_maximum_fusion.2), channel_id=1, source_target_pairs={{0,2},{2,0},{4,6},{6,4},{8,10},{10,8},{12,14},{14,12},{1,3},{3,1},... | collective-permute-start | bytes 393224 | tf_op jit(solution)/shard_map/ppermute | solution.py:192
  10.1 23.7 %collective-permute-start.15 = (bf16[16,4096]{1,0:T(8,128)(2,1)S(1)}, bf16[16,4096]{1,0:T(8,128)(2,1)S(1)}, u32[]{:S(2)}, u32[]{:S(2)}) collective-permute-start(bf16[16,4096]{1,0:T(8,128)(2,1)S(1)} %pad_maximum_fusion.2), channel_id=1, source_target_pairs={{0,16},{16,0},{1,17},{17,1},{2,18},{18,2},{3,19},{19,3},{4,20},{20... | collective-permute-start | bytes 393224 | tf_op jit(solution)/shard_map/ppermute | solution.py:192
  13.4 5.0 %collective-permute-start.4 = (bf16[16,4096]{1,0:T(8,128)(2,1)S(1)}, bf16[16,4096]{1,0:T(8,128)(2,1)S(1)}, u32[]{:S(2)}, u32[]{:S(2)}) collective-permute-start(bf16[16,4096]{1,0:T(8,128)(2,1)S(1)} %pad_maximum_fusion.3), channel_id=1, source_target_pairs={{0,4},{2,6},{4,0},{6,2},{8,12},{10,14},{12,8},{14,10},{1,5},{3,7},... | collective-permute-start | bytes 393224 | tf_op jit(solution)/shard_map/ppermute | solution.py:192
  19.0 7.1 %collective-permute-start.7 = (bf16[32,4096]{1,0:T(8,128)(2,1)S(1)}, bf16[32,4096]{1,0:T(8,128)(2,1)S(1)}, u32[]{:S(2)}, u32[]{:S(2)}) collective-permute-start(bf16[32,4096]{1,0:T(8,128)(2,1)S(1)} %constant_dynamic-update-slice_fusion), channel_id=1, source_target_pairs={{0,2},{2,0},{4,6},{6,4},{8,10},{10,8},{12,14},{14,12},{1,3},{3,1},... | collective-permute-start | bytes 786440 | tf_op jit(solution)/shard_map/ppermute | solution.py:192
  21.4 12.4 %collective-permute-start.16 = (bf16[32,4096]{1,0:T(8,128)(2,1)S(1)}, bf16[32,4096]{1,0:T(8,128)(2,1)S(1)}, u32[]{:S(2)}, u32[]{:S(2)}) collective-permute-start(bf16[32,4096]{1,0:T(8,128)(2,1)S(1)} %constant_dynamic-update-slice_fusion), channel_id=1, source_target_pairs={{0,16},{16,0},{1,17},{17,1},{2,18},{18,2},{3,19},{19,3},{4,20},{20... | collective-permute-start | bytes 786440 | tf_op jit(solution)/shard_map/ppermute | solution.py:192
  23.8 22.7 %collective-permute-start.10 = (bf16[16,2048]{1,0:T(8,128)(2,1)S(1)}, bf16[16,2048]{1,0:T(8,128)(2,1)S(1)}, u32[]{:S(2)}, u32[]{:S(2)}) collective-permute-start(bf16[16,2048]{1,0:T(8,128)(2,1)S(1)} %get-tuple-element.54), channel_id=1, source_target_pairs={{0,2},{2,0},{4,6},{6,4},{8,10},{10,8},{12,14},{14,12},{1,3},{3,1},... | collective-permute-start | bytes 196616 | tf_op jit(solution)/shard_map/ppermute | solution.py:192
  24.4 22.1 %collective-permute-start.6 = (bf16[32,2048]{1,0:T(8,128)(2,1)S(1)}, bf16[32,2048]{1,0:T(8,128)(2,1)S(1)}, u32[]{:S(2)}, u32[]{:S(2)}) collective-permute-start(bf16[32,2048]{1,0:T(8,128)(2,1)S(1)} %pad_maximum_fusion.4), channel_id=1, source_target_pairs={{0,4},{2,6},{4,0},{6,2},{8,12},{10,14},{12,8},{14,10},{1,5},{3,7},... | collective-permute-start | bytes 393224 | tf_op jit(solution)/shard_map/ppermute | solution.py:192
  26.1 5.0 %collective-permute-start.8 = (bf16[16,4096]{1,0:T(8,128)(2,1)S(1)}, bf16[16,4096]{1,0:T(8,128)(2,1)S(1)}, u32[]{:S(2)}, u32[]{:S(2)}) collective-permute-start(bf16[16,4096]{1,0:T(8,128)(2,1)S(1)} %collective-permute-done.4), channel_id=1, source_target_pairs={{0,2},{2,0},{4,6},{6,4},{8,10},{10,8},{12,14},{14,12},{1,3},{3,1},... | collective-permute-start | bytes 393224 | tf_op jit(solution)/shard_map/ppermute | solution.py:192
  31.0 7.2 %collective-permute-start.17 = (bf16[32,4096]{1,0:T(8,128)(2,1)S(1)}, bf16[32,4096]{1,0:T(8,128)(2,1)S(1)}, u32[]{:S(2)}, u32[]{:S(2)}) collective-permute-start(bf16[32,4096]{1,0:T(8,128)(2,1)S(1)} %pad_maximum_fusion.1), channel_id=1, source_target_pairs={{0,16},{16,0},{1,17},{17,1},{2,18},{18,2},{3,19},{19,3},{4,20},{20... | collective-permute-start | bytes 786440 | tf_op jit(solution)/shard_map/ppermute | solution.py:192
  38.9 20.0 %collective-permute-start.18 = (bf16[48,4096]{1,0:T(8,128)(2,1)S(1)}, bf16[48,4096]{1,0:T(8,128)(2,1)S(1)}, u32[]{:S(2)}, u32[]{:S(2)}) collective-permute-start(bf16[48,4096]{1,0:T(8,128)(2,1)S(1)} %get-tuple-element.42), channel_id=1, source_target_pairs={{0,16},{16,0},{1,17},{17,1},{2,18},{18,2},{3,19},{19,3},{4,20},{20... | collective-permute-start | bytes 1179656 | tf_op jit(solution)/shard_map/ppermute | solution.py:192
  42.3 4.3 %collective-permute-start.11 = (bf16[16,2048]{1,0:T(8,128)(2,1)S(1)}, bf16[16,2048]{1,0:T(8,128)(2,1)S(1)}, u32[]{:S(2)}, u32[]{:S(2)}) collective-permute-start(bf16[16,2048]{1,0:T(8,128)(2,1)S(1)} %get-tuple-element.38), channel_id=1, source_target_pairs={{0,2},{2,0},{4,6},{6,4},{8,10},{10,8},{12,14},{14,12},{1,3},{3,1},... | collective-permute-start | bytes 196616 | tf_op jit(solution)/shard_map/ppermute | solution.py:192
  43.9 5.9 %collective-permute-start.9 = (bf16[32,2048]{1,0:T(8,128)(2,1)S(1)}, bf16[32,2048]{1,0:T(8,128)(2,1)S(1)}, u32[]{:S(2)}, u32[]{:S(2)}) collective-permute-start(bf16[32,2048]{1,0:T(8,128)(2,1)S(1)} %pad_maximum_fusion.5), channel_id=1, source_target_pairs={{0,6},{2,4},{4,2},{6,0},{8,14},{10,12},{12,10},{14,8},{1,7},{3,5},... | collective-permute-start | bytes 393224 | tf_op jit(solution)/shard_map/ppermute | solution.py:192
  49.9 5.1 %collective-permute-start.12 = (bf16[8,2048]{1,0:T(8,128)(2,1)S(1)}, bf16[8,2048]{1,0:T(8,128)(2,1)S(1)}, u32[]{:S(2)}, u32[]{:S(2)}) collective-permute-start(bf16[8,2048]{1,0:T(8,128)(2,1)S(1)} %get-tuple-element.50), channel_id=1, source_target_pairs={{0,8},{1,9},{2,10},{3,11},{4,12},{5,13},{6,14},{7,15},{8,0},{9,1},... | collective-permute-start | bytes 98312 | tf_op jit(solution)/shard_map/ppermute | solution.py:209
  53.5 4.3 %collective-permute-start.14 = (bf16[8,2048]{1,0:T(8,128)(2,1)S(1)}, bf16[8,2048]{1,0:T(8,128)(2,1)S(1)}, u32[]{:S(2)}, u32[]{:S(2)}) collective-permute-start(bf16[8,2048]{1,0:T(8,128)(2,1)S(1)} %get-tuple-element.51), channel_id=1, source_target_pairs={{0,9},{1,8},{2,11},{3,10},{4,13},{5,12},{6,15},{7,14},{8,1},{9,0},... | collective-permute-start | bytes 98312 | tf_op jit(solution)/shard_map/ppermute | solution.py:209
  53.6 4.2 %collective-permute-start.13 = (bf16[8,2048]{1,0:T(8,128)(2,1)S(1)}, bf16[8,2048]{1,0:T(8,128)(2,1)S(1)}, u32[]{:S(2)}, u32[]{:S(2)}) collective-permute-start(bf16[8,2048]{1,0:T(8,128)(2,1)S(1)} %get-tuple-element.52), channel_id=1, source_target_pairs={{0,1},{1,0},{2,3},{3,2},{4,5},{5,4},{6,7},{7,6},{8,9},{9,8},{10,11... | collective-permute-start | bytes 98312 | tf_op jit(solution)/shard_map/ppermute | solution.py:192
